TPU v7x, 32 devices: a whole 2x2x4 slice. The times are simulated.
32 devices in a mesh: dp: 8 (over z, x), mp: 4 (over y, core).
Axes of the slice: x: 2, y: 2, z: 4, core: 2. Of those that a mesh axis runs over, the one named last changes fastest.
Arguments:
- tokens: bfloat16 [2, 16384, 768], P(None, ('dp', 'mp')), may hold values from -6 to 6
- norm_gains: bfloat16 [768, 2], P('dp'), may hold values from 0.5 to 1.5
- norm_biases: bfloat16 [768, 2], P('dp'), may hold values from -3 to 3
- w_query: bfloat16 [768, 768], P('dp', 'mp'), may hold values from -0.21875 to 0.21875
- w_keyval: bfloat16 [768, 128], P('dp'), may hold values from -0.21875 to 0.21875
- w_output: bfloat16 [768, 768], P('dp', 'mp'), may hold values from -1.5 to 1.5
- w_up: bfloat16 [768, 3072], P('dp', 'mp'), may hold values from -0.21875 to 0.21875
- w_down: bfloat16 [768, 3072], P('dp', 'mp'), may hold values from -0.109375 to 0.109375
- cotangent: bfloat16 [2, 16384, 768], P(None, ('dp', 'mp')), may hold values from -6 to 6
- subset_ids: int32 [32768], P('dp'), may hold values from 0 to 21
- subset_weights: float32 [22], replicated, may hold values from 0.25 to 4
Outputs:
- output: bfloat16 [2, 16384, 768], P(None, ('dp', 'mp'))
- kv_cache: bfloat16 [32768, 128], P('dp')
- input_grad: bfloat16 [2, 16384, 768], P(None, ('dp', 'mp'))
- grad_gains: float32 [768, 2], P('dp')
- grad_biases: float32 [768, 2], P('dp')
- grad_query: float32 [768, 768], P('dp', 'mp')
- grad_keyval: float32 [768, 128], P('dp')
- grad_output: float32 [768, 768], P('dp', 'mp')
- grad_up: float32 [768, 3072], P('dp', 'mp')
- grad_down: float32 [768, 3072], P('dp', 'mp')
All inputs are finite; a program needn't handle non-finite values.
Results may differ from a plain program's by a relative error of at most 0.012.
Values may be sent and summed in bfloat16 or wider, within the bound.
A program may use at most 256 MiB of HBM per device.

v0:
```python
import functools

import jax
import jax.numpy as jnp
from jax import lax
from jax.experimental import pallas as pl
from jax.experimental.pallas import tpu as pltpu
from jax.sharding import PartitionSpec as P

f32 = jnp.float32
bf = jnp.bfloat16
MESH = pl.DeviceIdType.MESH
HD = 64
ROT = 16
B = 512
SEQ_LEN = 2048
epsilon = 1e-05
sqrt_half = 0.7071067811865476
inv_sqrt_two_pi = 0.3989422804014327


def coords(nz):
    d=lax.axis_index("dp"); m=lax.axis_index("mp")
    return d//2, d%2, m//2, m%2

def peer(pos,kind,nz):
    z,x,y,c=pos
    if kind[0]=="z": z=lax.rem(z+int(kind[1:]),nz)
    if kind=="x": x=1-x
    if kind=="y": y=1-y
    if kind=="c": c=1-c
    return (z*2+x, y*2+c)

def greet(pos,kinds,nz):
    bar=pltpu.get_barrier_semaphore()
    for k in kinds:
        pl.semaphore_signal(bar,inc=1,device_id=peer(pos,k,nz),device_id_type=MESH)
    pl.semaphore_wait(bar,len(kinds))

def gather_routes(order,nz):
    zs=[f"z{k}" for k in range(1,nz)]
    out=[]
    if order=="zyx":
        out.append(((0,0,0),zs+["y","x","c"]))
        out+=[((k,0,0),["y","x","c"]) for k in range(1,nz)]
        out+=[((k,0,1),["x","c"]) for k in range(nz)]
        out+=[((k,1,r),["c"]) for r in (0,1) for k in range(nz)]
    elif order=="xzy":
        out.append(((0,0,0),["x"]+zs+["y","c"]))
        out.append(((0,1,0),zs+["y","c"]))
        out+=[((k,r,0),["y","c"]) for k in range(1,nz) for r in (0,1)]
        out+=[((k,r,1),["c"]) for k in range(nz) for r in (0,1)]
    elif order=="zx":
        out.append(((0,0,0),zs+["x"]))
        out+=[((k,0,0),["x"]) for k in range(1,nz)]
        out+=[((k,1,0),[]) for k in range(nz)]
    return out

def columns(m,w,lo,hi):
    return pl.ds(pl.multiple_of(m*w+lo,128),hi-lo)

class Gather:
    late=0.42
    def __init__(self,shards,plan,dp,mp):
        self.plan=plan; self.nz=dp//2; self.mp=mp; self.dp=dp
        inside={i for i,_,_,o in plan if o=="zx"}
        self.ins=[pl.BlockSpec(memory_space=pltpu.VMEM)]*len(shards)
        self.outs=[pl.BlockSpec(memory_space=pl.ANY)]*len(shards)
        self.shapes=[jax.ShapeDtypeStruct((dp,s.shape[0],s.shape[1]*(1 if i in inside else mp)),s.dtype) for i,s in enumerate(shards)]
        sends=sum(len(f) for _,_,_,o in plan for _,f in gather_routes(o,self.nz))
        self.scratch=[pltpu.SemaphoreType.DMA((sends,)),pltpu.SemaphoreType.DMA((len(plan),mp,dp)),pltpu.SemaphoreType.DMA((len(shards),))]
    def build(self,pos,shards,full,scr):
        send,recv,local=scr
        nz=self.nz; z,x,y,c=pos
        routes=[gather_routes(o,nz) for _,_,_,o in self.plan]
        sent=[]
        def where(p,rel,other):
            i,lo,hi,order=self.plan[p]; k,rx,ry=rel
            zz=lax.rem(z+nz-k,nz); xx=1-x if rx else x; yy=1-y if ry else y
            d=zz*2+xx; m=yy*2+(1-c if other else c)
            if order=="zx": return full[i].at[d,:,lo:hi],recv.at[p,0,d]
            return full[i].at[d,:,columns(m,shards[i].shape[1],lo,hi)],recv.at[p,m,d]
        def arrived(p,rel,other):
            dst,sem=where(p,rel,other)
            pltpu.make_async_remote_copy(dst,dst,send.at[0],sem,device_id=peer(pos,"c",nz),device_id_type=MESH).wait_recv()
        def copy(p,rel,f,own,n):
            i,lo,hi,_=self.plan[p]
            dst,sem=where(p,rel,False)
            src=shards[i].at[:,lo:hi] if own else dst
            return pltpu.make_async_remote_copy(src,dst,send.at[n],sem,device_id=peer(pos,f,nz),device_id_type=MESH)
        def step(p,s):
            rel,fw=routes[p][s]
            base=len(sent)
            cps=[functools.partial(copy,p,rel,f,s==0,base+j) for j,f in enumerate(fw)]
            sent.extend(cps)
            def go():
                if s: arrived(p,rel,False)
                for cp in cps: cp().start()
            return go
        def mine(i):
            order=[o for j,_,_,o in self.plan if j==i][0]
            d=z*2+x; w=shards[i].shape[1]
            dst=full[i].at[d] if order=="zx" else full[i].at[d,:,columns(y*2+c,w,0,w)]
            return pltpu.make_async_copy(shards[i],dst,local.at[i])
        first=[step(p,0) for p in range(len(self.plan))]
        steps=[]
        longest=max(len(r) for r in routes)
        for s in range(1,longest):
            for p,r in enumerate(routes):
                if s<len(r): steps.append(((s-1)/(longest-1),step(p,s)))
        def begin():
            for g in first: g()
            for i in range(len(shards)): mine(i).start()
        def end():
            for p,r in enumerate(routes):
                if self.plan[p][3]=="zx": continue
                for rel,_ in r: arrived(p,rel,True)
            for cp in sent: cp().wait_send()
            for i in range(len(shards)): mine(i).wait()
        return begin,steps,end

class Scatter:
    loop=False
    late=0.0
    def __init__(self,parts,plan,dp,mp):
        self.plan=plan; nz=self.nz=dp//2; self.mp=mp
        self.width=[]
        for i,p in enumerate(parts):
            inside=[o for j,_,_,o in plan if j==i][0]=="xz"
            self.width.append(p.shape[-1]//(1 if inside else mp))
        self.ins=[pl.BlockSpec(memory_space=pl.ANY)]*len(parts)
        self.outs=[pl.BlockSpec(memory_space=pltpu.VMEM)]*len(parts)
        self.shapes=[jax.ShapeDtypeStruct((p.shape[1],w),f32) for p,w in zip(parts,self.width)]
        scr=[]; sends=0
        for i,lo,hi,order in plan:
            rows=parts[i].shape[1]; w=hi-lo
            b=lambda k: pltpu.VMEM((k,rows,w),bf)
            nb=nz*4 if order!="xz" else nz*2
            scr+=[b(nb),b(nb)]
            if order=="xyz": scr+=[b(nz*2),b(nz),b(nz)]; sends+=nb+2*nz+nz+nz-1
            elif order=="yzx": scr+=[b(1),b(nz*2),b(nz*2)]; sends+=nb+2*nz+2*(nz-1)+1
            else: scr+=[b(nz*2),b(nz),b(2*nz)]; sends+=nb+nz+nz+nz-1
        n=len(plan)
        self.scratch=scr+[pltpu.SemaphoreType.DMA((n,4*nz)),pltpu.SemaphoreType.DMA((sends,)),pltpu.SemaphoreType.DMA((n,4*nz)),pltpu.SemaphoreType.DMA((n,2*nz)),pltpu.SemaphoreType.DMA((n,2*nz)),pltpu.SemaphoreType.DMA((n,2*nz))]
    def build(self,pos,parts,outs,scr):
        plan=self.plan; nz=self.nz; z,x,y,c=pos; n=len(plan)
        per=scr[:5*n]; own,send,csem,xsem,ysem,zsem=scr[5*n:]
        sent=[]; begins=[]; steps=[]; ends=[]
        def sender(src,dst,rsem,kind):
            k=len(sent)
            cp=lambda: pltpu.make_async_remote_copy(src(),dst,send.at[k],rsem,device_id=peer(pos,kind,nz),device_id_type=MESH)
            sent.append(cp)
            return lambda: cp().start()
        def wait(dst,rsem):
            pltpu.make_async_remote_copy(dst,dst,send.at[0],rsem,device_id=peer(pos,"c",nz),device_id_type=MESH).wait_recv()
        def part(p,r,cc):
            i,lo,hi,order=plan[p]
            rz,rx,ry=r
            zz=lax.rem(z+rz,nz); xx=1-x if rx else x; yy=1-y if ry else y
            if order=="xz": return parts[i].at[zz*2+xx,:,lo:hi]
            return parts[i].at[zz*2+xx,:,columns(yy*2+cc,self.width[i],lo,hi)]
        def total(dst,*refs):
            step=32 if self.loop and dst.shape[0]%32==0 else dst.shape[0]
            def body(r,carry):
                w=pl.ds(pl.multiple_of(r*step,step),step)
                v=refs[0][w,:].astype(f32)
                for o in refs[1:]: v=v+o[w,:].astype(f32)
                dst[w,:]=v.astype(dst.dtype)
                return carry
            if step==dst.shape[0]: body(0,0)
            else: lax.fori_loop(0,dst.shape[0]//step,body,0)
        down=range(nz-1,-1,-1)
        for p,(i,lo,hi,order) in enumerate(plan):
            acc,cb,xb,yb,zb=per[5*p:5*p+5]
            if order=="xyz": seq=[(k,1,r) for r in (1,0) for k in down]+[(k,0,1) for k in down]+[(k,0,0) for k in down]
            elif order=="yzx": seq=[(k,r,1) for r in (1,0) for k in down]+[(k,1,0) for k in down]+[(k,0,0) for k in down]
            else: seq=[(k,1,0) for k in down]+[(k,0,0) for k in down]
            slot=(lambda r: (r[0]*2+r[1])*2+r[2]) if order!="xz" else (lambda r: r[0]*2+r[1])
            A=lambda r,acc=acc,slot=slot: acc.at[slot(r)]
            def plus(when,p=p):
                def note(f): steps.append((when,f))
                return note
            for t,r in enumerate(seq):
                s=slot(r); rz,rx,ry=r
                begins.append((t,sender(functools.partial(part,p,r,c if order=="xz" else 1-c),cb.at[s],csem.at[p,s],"c")))
                mine=lambda p=p,r=r,s=s,acc=acc: pltpu.make_async_copy(part(p,r,c),acc.at[s],own.at[p,s])
                begins.append((t,lambda mine=mine: mine().start()))
                go=None
                if order in ("xyz","xz") and rx: go=sender(lambda v=A(r): v,xb.at[rz*2+ry],xsem.at[p,rz*2+ry],"x")
                if order=="yzx" and ry: go=sender(lambda v=A(r): v,yb.at[rz*2+rx],ysem.at[p,rz*2+rx],"y")
                @plus(0.22*t/len(seq))
                def _(p=p,s=s,acc=acc,cb=cb,go=go,mine=mine):
                    mine().wait()
                    wait(cb.at[s],csem.at[p,s])
                    total(acc.at[s],acc.at[s],cb.at[s])
                    if go: go()
            if order=="xyz":
                for n_,k in enumerate(down):
                    r=(k,0,1); j=k*2+1
                    go=sender(lambda v=A(r): v,yb.at[k],ysem.at[p,k],"y")
                    @plus(0.24+0.26*n_/nz)
                    def _(p=p,r=r,j=j,A=A,xb=xb,go=go):
                        wait(xb.at[j],xsem.at[p,j]); total(A(r),A(r),xb.at[j])
                        go()
                for n_,k in enumerate(down):
                    r=(k,0,0); j=k*2
                    go=sender(lambda v=A(r): v,zb.at[k],zsem.at[p,k],f"z{k}") if k else None
                    @plus(0.52+0.26*n_/nz)
                    def _(p=p,r=r,j=j,k=k,A=A,xb=xb,yb=yb,go=go):
                        wait(xb.at[j],xsem.at[p,j]); wait(yb.at[k],ysem.at[p,k])
                        if go:
                            total(A(r),A(r),xb.at[j],yb.at[k])
                            go()
                def fin(p=p,i=i,lo=lo,hi=hi,A=A,xb=xb,yb=yb,zb=zb):
                    for k in range(1,nz): wait(zb.at[k],zsem.at[p,k])
                    total(outs[i].at[:,lo:hi],A((0,0,0)),xb.at[0],yb.at[0],*[zb.at[k] for k in range(1,nz)])
                ends.append(fin)
            elif order=="yzx":
                for n_,(rx,k) in enumerate([(rx,k) for rx in (1,0) for k in range(nz-1,0,-1)]):
                    r=(k,rx,0); j=k*2+rx
                    go=sender(lambda v=A(r): v,zb.at[k*2+rx],zsem.at[p,k*2+rx],f"z{k}")
                    @plus(0.24+0.3*n_/(2*nz-2))
                    def _(p=p,r=r,j=j,A=A,yb=yb,go=go):
                        wait(yb.at[j],ysem.at[p,j]); total(A(r),A(r),yb.at[j])
                        go()
                r=(0,1,0)
                go=sender(lambda v=A(r): v,xb.at[0],xsem.at[p,0],"x")
                @plus(0.8)
                def _(p=p,r=r,A=A,yb=yb,zb=zb,go=go):
                    wait(yb.at[1],ysem.at[p,1])
                    for k in range(1,nz): wait(zb.at[k*2+1],zsem.at[p,k*2+1])
                    total(A(r),A(r),yb.at[1],*[zb.at[k*2+1] for k in range(1,nz)])
                    go()
                def fin(p=p,i=i,lo=lo,hi=hi,A=A,xb=xb,yb=yb,zb=zb):
                    wait(yb.at[0],ysem.at[p,0])
                    for k in range(1,nz): wait(zb.at[k*2],zsem.at[p,k*2])
                    wait(xb.at[0],xsem.at[p,0])
                    total(outs[i].at[:,lo:hi],A((0,0,0)),yb.at[0],xb.at[0],*[zb.at[k*2] for k in range(1,nz)])
                ends.append(fin)
            else:
                for n_,k in enumerate(down):
                    r=(k,0,0)
                    go=sender(lambda v=A(r): v,yb.at[k],ysem.at[p,k],"y")
                    @plus(0.24+0.26*n_/nz)
                    def _(p=p,r=r,k=k,A=A,xb=xb,go=go):
                        wait(xb.at[k*2],xsem.at[p,k*2]); total(A(r),A(r),xb.at[k*2])
                        go()
                for n_,k in enumerate(range(nz-1,0,-1)):
                    go=sender(lambda v=zb.at[k]: v,zb.at[nz+k],zsem.at[p,k],f"z{k}")
                    @plus(0.52+0.26*n_/nz)
                    def _(p=p,k=k,A=A,yb=yb,zb=zb,go=go):
                        wait(yb.at[k],ysem.at[p,k]); total(zb.at[k],A((k,0,0)),yb.at[k])
                        go()
                def fin(p=p,i=i,lo=lo,hi=hi,A=A,yb=yb,zb=zb):
                    wait(yb.at[0],ysem.at[p,0])
                    for k in range(1,nz): wait(zb.at[nz+k],zsem.at[p,k])
                    total(outs[i].at[:,lo:hi],A((0,0,0)),yb.at[0],*[zb.at[nz+k] for k in range(1,nz)])
                ends.append(fin)
        begins.sort(key=lambda e: e[0])
        steps.sort(key=lambda e: e[0])
        def begin():
            for _,g in begins: g()
        def end():
            for f in ends: f()
            for cp in sent: cp().wait_send()
        return begin,steps,end

def scatter_kernel(nz,comm,*refs):
    gq_ref,go_ref,sums_ref,scale_ref=refs[:4]
    hosted=refs[4:11]
    outq_ref,outo_ref,outkv_ref,outgb_ref,out_hbm,ig_hbm=refs[11:17]
    refs=refs[17:]
    qo,kvg,a_ref,c_ref,out_ref,ig_ref,osem=refs[:7]
    refs=refs[7:]
    o_ref,wo_ref,hid_ref,down_ref,tok_ref,cot_ref,dn_ref=refs[:7]
    fetch=[pltpu.make_async_copy(h,v,refs[7].at[k]) for k,(h,v) in enumerate(zip(hosted,refs[:7]))]
    for f in fetch: f.start()
    pos=coords(nz)
    greet(pos,[f"z{k}" for k in range(1,nz)]+["x","y","c"],nz)
    rows=gq_ref.shape[1]
    lane=lax.broadcasted_iota(jnp.int32,(rows,128),1)<64
    def tile(ref,d,h): return ref[d,:,128*(h//2):128*(h//2)+128].astype(f32)
    def pack(d,carry):
        for t in range(qo.shape[2]//128):
            m,k=t//3,t%3
            lo,hi=[((gq_ref,3*m),(gq_ref,3*m+1)),((gq_ref,3*m+2),(go_ref,3*m)),((go_ref,3*m+1),(go_ref,3*m+2))][k]
            qo[d,:,128*t:128*t+128]=halves(tile(lo[0],d,lo[1]),lo[1]%2,tile(hi[0],d,hi[1]),hi[1]%2,lane).astype(bf)
        return carry
    lax.fori_loop(0,qo.shape[0],pack,0)
    s=jnp.concatenate([sums_ref[...],jnp.zeros((120,sums_ref.shape[1]),f32)],axis=0).T
    for d in range(kvg.shape[0]):
        kvg[d,:,:128]=gq_ref[d,:,gq_ref.shape[2]-128:]
        kvg[d,:,128:]=s[rows*d:rows*d+rows].astype(bf)
    begin,steps,end=comm.build(pos,(qo,kvg),(a_ref,c_ref),refs[8:])
    begin()
    T=256
    def leave(k,r):
        rows=pl.ds(pl.multiple_of(r*T,T),T)
        src,dst=((out_ref,out_hbm),(ig_ref,ig_hbm))[k]
        return pltpu.make_async_copy(src.at[rows,:],dst.at[rows,:],osem.at[k,r])
    across=out_ref.shape[1]//T; n=out_ref.shape[0]//T*across
    slots=[[] for _ in range(n)]
    for when,s in steps:
        if when<0.23: s()
        else: slots[min(n-1,int(n*(0.33+(when-0.24)*1.15)))].append(s)
    def chunk(it,carry):
        rows=pl.ds(pl.multiple_of(it//across*T,T),T); cols=pl.ds(pl.multiple_of(it%across*T,T),T)
        @pl.when(it%across==0)
        def _():
            v=tok_ref[rows,:].astype(f32)
            v=v-jnp.mean(v,axis=1,keepdims=True)
            inverse=lax.rsqrt(jnp.mean(v*v,axis=1,keepdims=True)+epsilon)
            v=v*inverse
            dn=dn_ref[rows,:]
            dx=(dn-jnp.mean(dn,axis=1,keepdims=True)-v*jnp.mean(dn*v,axis=1,keepdims=True))*inverse
            ig_ref[rows,:]=(cot_ref[rows,:].astype(f32)*scale_ref[rows,:]+dx).astype(bf)
        y=tok_ref[rows,cols].astype(f32)+dg(o_ref[rows,:],wo_ref[cols,:],NT)+dg(hid_ref[rows,:],down_ref[cols,:],NT)
        out_ref[rows,cols]=y.astype(bf)
        @pl.when(it%across==across-1)
        def _():
            for k in range(2): leave(k,it//across).start()
        for k in range(n):
            if slots[k]:
                @pl.when(it==k)
                def _(k=k):
                    for s in slots[k]: s()
        return carry
    for f in fetch: f.wait()
    lax.fori_loop(0,n,chunk,0)
    end()
    a=a_ref[...]; half=a.shape[1]//2
    outq_ref[...]=a[:,:half]; outo_ref[...]=a[:,half:]
    outkv_ref[...]=c_ref[:,:128]
    outgb_ref[...]=c_ref[:,128:].T[:8]
    for r in range(n//across):
        for k in range(2): leave(k,r).wait()

def halves(lo,lo_at,hi,hi_at,lane):
    if lo_at: lo=pltpu.roll(lo,64,1)
    if not hi_at: hi=pltpu.roll(hi,64,1)
    return jnp.where(lane,lo,hi)

def scatter_small(gq,go,sums,o,wo,hidden,down,tokens,cotangent,scale,dnormed,dp,mp,cid):
    hosted=(o,wo,hidden,down,tokens,cotangent,dnormed)
    part=gq.shape[1]; cols=go.shape[2]//mp
    shape=lambda w: jax.ShapeDtypeStruct((dp,gq.shape[1],w),bf)
    qo,kvg=shape(2*go.shape[2]),shape(256)
    comm=Scatter([qo,kvg],[(1,0,256,"xz"),(0,0,256,"xyz"),(0,256,384,"yzx")],dp,mp)
    comm.loop=True
    vm=pl.BlockSpec(memory_space=pltpu.VMEM)
    return pl.pallas_call(functools.partial(scatter_kernel,comm.nz,comm),
        in_specs=[vm]*4+[pl.BlockSpec(memory_space=pl.ANY)]*len(hosted),out_specs=[vm]*4+[pl.BlockSpec(memory_space=pl.ANY)]*2,
        out_shape=[jax.ShapeDtypeStruct(d,f32) for d in ((part,cols),(part,cols),(part,128),(8,part))]+[jax.ShapeDtypeStruct(o.shape,bf)]*2,
        scratch_shapes=[pltpu.VMEM(qo.shape,bf),pltpu.VMEM(kvg.shape,bf),pltpu.VMEM((part,2*cols),f32),pltpu.VMEM((part,256),f32),pltpu.VMEM(o.shape,bf),pltpu.VMEM(o.shape,bf),pltpu.SemaphoreType.DMA((2,o.shape[0]//256))]+[pltpu.VMEM(h.shape,h.dtype) for h in hosted]+[pltpu.SemaphoreType.DMA((len(hosted),))]+comm.scratch,
        compiler_params=pltpu.CompilerParams(collective_id=cid,has_side_effects=True,vmem_limit_bytes=60<<20),name="scatter_grads")(gq,go,sums,scale,*hosted)

def prologue_kernel(nz,comms,*refs):
    tok_ref,cos_ref,sin_ref,wq_ref,wo_ref,wkv_ref,gain_ref,bias_ref=refs[:8]
    q_out,o_out,small_out,normed_out,ain_out,min_out,kv_out,all_out=refs[8:16]
    qo_own,kvg_own,qo_full,kvg_full,wkv_scr,ksend,krecv=refs[16:23]
    pos=coords(nz); z,x,y,c=pos
    greet(pos,[f"z{k}" for k in range(1,nz)]+["x","y","c"],nz)
    rows=wq_ref.shape[0]
    kvg_own[:,:128]=wkv_ref[...]
    kvg_own[:,128:]=jnp.concatenate([gain_ref[...].astype(f32),bias_ref[...].astype(f32),jnp.zeros((124,rows),f32)],axis=0).T.astype(bf)
    g,b=comms
    ga=g.build(pos,(kvg_own,),(kvg_full,),refs[23:26])
    gb=b.build(pos,(qo_own,),(qo_full,),refs[26:29])
    ga[0]()
    wq=wq_ref[...].astype(f32); wo=wo_ref[...].astype(f32)
    qo_own[:,:128]=wq[:,:128].astype(bf)
    qo_own[:,128:256]=jnp.concatenate([wq[:,128:],wo[:,:64]],axis=1).astype(bf)
    qo_own[:,256:]=wo[:,64:].astype(bf)
    gb[0]()
    nb,own,width=tok_ref.shape
    part=own//4
    def norm(k,carry):
        v=tok_ref[k//4,pl.ds(pl.multiple_of(k%4*part,part),part),:].astype(f32)
        v=v-jnp.mean(v,axis=1,keepdims=True)
        normed_out[pl.ds(pl.multiple_of(k*part,part),part),:]=v*lax.rsqrt(jnp.mean(v*v,axis=1,keepdims=True)+epsilon)
        return carry
    lax.fori_loop(0,4*nb,norm,0)
    sa=[s for _,s in ga[1]]; sb=[s for _,s in gb[1]]
    while sa:
        sa.pop(0)()
        if sb: sb.pop(0)()
    ga[2]()
    kvg=kvg_full[...].reshape(width,256)
    small=kvg[:,128:].astype(f32).T
    small_out[...]=small[:8]
    wkv=kvg[:,:128]
    for d in range(q_out.shape[0]): all_out[d,:,width:]=kvg_full[d,:,:128]
    wkv_scr[...]=wkv
    def copy(s,m,src,kind,n):
        return pltpu.make_async_remote_copy(src,kv_out.at[s,m],ksend.at[n],krecv.at[s,m],device_id=peer(pos,kind,nz),device_id_type=MESH)
    copies=[]
    me=y*2+c
    for s in range(nb):
        def project(k,carry):
            w=pl.ds(pl.multiple_of(k*part,part),part); rows=pl.ds(pl.multiple_of(s*own+k*part,part),part)
            ain=(normed_out[rows,:]*small[0:1]+small[2:3]).astype(bf)
            ain_out[rows,:]=ain
            kv_out[s,me,w,:]=turn(dg(ain,wkv_scr[...],NN),cos_ref[w,:],sin_ref[w,:],False,True).astype(bf)
            return carry
        lax.fori_loop(0,4,project,0)
        for kind in ("y","c"):
            cp=copy(s,me,kv_out.at[s,me],kind,len(copies)); cp.start(); copies.append(cp)
        def feed(k,carry):
            rows=pl.ds(pl.multiple_of(s*own+k*part,part),part)
            min_out[rows,:]=(normed_out[rows,:]*small[1:2]+small[3:4]).astype(bf)
            return carry
        lax.fori_loop(0,4,feed,0)
        for _ in range(6):
            if sb: sb.pop(0)()
    other=(1-y)*2+c
    for s in range(nb):
        copy(s,other,kv_out.at[s,other],"c",0).wait_recv()
        cp=copy(s,other,kv_out.at[s,other],"c",len(copies)); cp.start(); copies.append(cp)
    for s in sb: s()
    gb[2]()
    lane=lax.broadcasted_iota(jnp.int32,(rows,128),1)<64
    def unpack(d,carry):
        def tile(m,k): return qo_full[d,:,384*m+128*k:384*m+128*k+128].astype(f32)
        for ref,place in ((q_out,[(0,0),(0,1),(1,0)]),(o_out,[(1,1),(2,0),(2,1)])):
            for j in range(ref.shape[2]//128):
                (m0,(k0,h0)),(m1,(k1,h1))=[(h//3,place[h%3]) for h in (2*j,2*j+1)]
                t=halves(tile(m0,k0),h0,tile(m1,k1),h1,lane).astype(bf)
                ref[d,:,128*j:128*j+128]=t
                if ref is q_out: all_out[d,:,128*j:128*j+128]=t
        return carry
    lax.fori_loop(0,q_out.shape[0],unpack,0)
    for s in range(nb):
        for m in (y*2+1-c,(1-y)*2+1-c): copy(s,m,kv_out.at[s,m],"c",0).wait_recv()
    for cp in copies: cp.wait_send()

def prologue(tokens,cos,sin,wq,wo,wkv,gains,biases,dp,mp,cid):
    nb,own,width=tokens.shape; part,cols=wq.shape
    kvg=jax.ShapeDtypeStruct((part,256),bf); qo=jax.ShapeDtypeStruct((part,2*cols),bf)
    comms=(Gather([kvg],[(0,0,256,"zx")],dp,mp),Gather([qo],[(0,0,256,"zyx"),(0,256,384,"xzy")],dp,mp))
    vm=pl.BlockSpec(memory_space=pltpu.VMEM)
    s=lambda *a: jax.ShapeDtypeStruct(a,bf)
    return pl.pallas_call(functools.partial(prologue_kernel,dp//2,comms),
        in_specs=[vm]*8,out_specs=[vm]*8,
        out_shape=[s(dp,part,width),s(dp,part,width),jax.ShapeDtypeStruct((8,width),f32),jax.ShapeDtypeStruct((nb*own,width),f32),s(nb*own,width),s(nb*own,width),s(nb,mp,own,128),s(dp,part,width+128)],
        scratch_shapes=[pltpu.VMEM(qo.shape,bf),pltpu.VMEM(kvg.shape,bf),pltpu.VMEM((dp,part,mp*2*cols),bf),pltpu.VMEM((dp,part,256),bf),pltpu.VMEM((width,128),bf),
                        pltpu.SemaphoreType.DMA((3*nb,)),pltpu.SemaphoreType.DMA((nb,mp))]+comms[0].scratch+comms[1].scratch,
        compiler_params=pltpu.CompilerParams(collective_id=cid,has_side_effects=True,vmem_limit_bytes=60<<20),name="gather_weights")(tokens,cos,sin,wq,wo,wkv,gains.T,biases.T)

NT=(((1,),(1,)),((),()))
NN=(((1,),(0,)),((),()))
def dg(a,b,dn): return lax.dot_general(a,b,dn,preferred_element_type=f32)
def turn(v,cos,sin,back,keys_only=False):
    lane=lax.broadcasted_iota(jnp.int32,v.shape,1)
    other=jnp.where(lane%HD<ROT//2,-pltpu.roll(v,128-ROT//2,1),pltpu.roll(v,ROT//2,1))*sin
    w=v*cos-other if back else v*cos+other
    return jnp.where(lane<HD,w,v) if keys_only else w

class Fold:
    scratch=[pltpu.VMEM((2,2,B,128),bf),pltpu.VMEM((2,2,B,128),bf),pltpu.VMEM((2,B,128),bf),pltpu.VMEM((2,B,128),bf),
             pltpu.SemaphoreType.DMA((6,)),pltpu.SemaphoreType.DMA((2,2)),pltpu.SemaphoreType.DMA((2,))]
    def __init__(self,pos,nz,out,cos,sin,scr):
        self.pos=pos; self.nz=nz; self.out=out; self.cos=cos; self.sin=sin; self.scr=scr
    def copy(self,b,n,src,dst,sem,kind):
        return pltpu.make_async_remote_copy(src,dst,self.scr[4].at[3*b+n],sem,device_id=peer(self.pos,kind,self.nz),device_id_type=MESH)
    def across(self,b,ry):
        low,cbuf=self.scr[:2]
        return self.copy(b,ry,low.at[b,ry],cbuf.at[b,ry],self.scr[5].at[b,ry],"c")
    def far(self,b):
        _,_,ybuf,ysend=self.scr[:4]
        return self.copy(b,2,ysend.at[b],ybuf.at[b],self.scr[6].at[b],"y")
    def one(self,b,part):
        _,_,y,c=self.pos
        for ry in (1,0):
            self.scr[0][b,ry]=part((1-y if ry else y)*2+1-c).astype(bf)
            self.across(b,ry).start()
    def two(self,b,part):
        _,_,y,c=self.pos
        self.across(b,1).wait_recv()
        self.scr[3][b]=(part((1-y)*2+c)+self.scr[1][b,1].astype(f32)).astype(bf)
        self.far(b).start()
    def three(self,b,part):
        _,_,y,c=self.pos
        self.across(b,0).wait_recv(); self.far(b).wait_recv()
        v=part(y*2+c)+self.scr[1][b,0].astype(f32)+self.scr[2][b].astype(f32)
        self.out[b*B:b*B+B,self.out.shape[1]-128:]=turn(v,self.cos[...],self.sin[...],True,True).astype(bf)
        self.across(b,1).wait_send(); self.across(b,0).wait_send(); self.far(b).wait_send()

def attn_kernel(nz,pairs,comm,join,nc,*refs):
    q_ref,do_ref,kv_ref,cos_ref,sin_ref=refs[:5]
    refs=refs[5:]
    if join: prev,refs=refs[:3],refs[3:]
    cin=refs[:nc]
    o_ref,dq_ref=refs[nc:2+nc]
    refs=refs[2+nc:]
    if not join: dkv_ref,refs=refs[0],refs[1:]
    cout=refs[:nc]
    k2,v2,kvt,acck,accv,ps,mk,ms,ls,ots,dqs=refs[nc:11+nc]
    refs=refs[11+nc:]
    rb=lax.axis_index("mp")
    nkb=kv_ref.shape[1]//B
    at=0
    if join:
        dkvs,local,fold,refs=refs[0],refs[1],refs[2:9],refs[9:]
        at=B
        part0=lambda m: prev[2][0,pl.ds(pl.multiple_of(m*B,B),B),:]
        part1=lambda m: dkvs[m]
    own=slice(at,at+B)
    slots=[[] for _ in range(pairs*2*nkb)]
    if comm:
        pos=coords(nz)
        greet(pos,[f"z{k}" for k in range(1,nz)]+["x","y","c"],nz)
        begin,steps,end=comm.build(pos,cin,cout,refs)
        begin()
        for when,s in steps: slots[int((comm.late+(1-comm.late)*when)*len(slots))].append(s)
        if join:
            sums=Fold(pos,nz,dq_ref,cos_ref,sin_ref,fold)
            sums.one(0,part0)
            slots[len(slots)//6].append(lambda: sums.two(0,part0))
            slots[len(slots)//2].append(lambda: sums.three(0,part0))
            before=[pltpu.make_async_copy(prev[k],r.at[:B,:prev[k].shape[1]],local.at[k]) for k,r in enumerate((o_ref,dq_ref))]
            for cp in before: cp.start()
    def between(pair,kb,base):
        for p in range(pairs):
            todo=[k for k in range(nkb) if slots[(2*p+base)*nkb+k]]
            if not todo: continue
            @pl.when(pair==p)
            def _(p=p,todo=todo):
                for k in todo:
                    @pl.when(kb==k)
                    def _(k=k):
                        for s in slots[(2*p+base)*nkb+k]: s()
    lane=lax.broadcasted_iota(jnp.int32,(B,128),1)<64
    def setup(kb,carry):
        kv=kv_ref[0,pl.ds(pl.multiple_of(kb*B,B),B),:].astype(f32)
        rolled=pltpu.roll(kv,64,1)
        k2[kb]=jnp.where(lane,kv,rolled).astype(bf)
        v2[kb]=jnp.where(lane,rolled,kv).astype(bf)
        kvt[kb]=kv.T.astype(bf)
        acck[kb]=jnp.zeros((B,128),f32); accv[kb]=jnp.zeros((B,128),f32)
        return carry
    lax.fori_loop(0,nkb,setup,0)
    def one(pair,carry):
        cols=pl.ds(pl.multiple_of(pair*128,128),128)
        q=(turn(q_ref[:,cols],cos_ref[...],sin_ref[...],False)*HD**-0.5).astype(bf); do=do_ref[:,cols]
        zero=jnp.zeros_like(q)
        qm=(jnp.where(lane,q,zero),jnp.where(lane,zero,q))
        dom=(jnp.where(lane,do,zero),jnp.where(lane,zero,do))
        ms[...]=jnp.full_like(ms,-1e30); ls[...]=jnp.zeros_like(ls)
        ots[...]=jnp.zeros_like(ots); dqs[...]=jnp.zeros_like(dqs)
        H=range(2)
        def fwd(kb,masked):
            ss=[dg(k2[kb],qm[h],NT) for h in H]
            if masked:
                ki=lax.broadcasted_iota(jnp.int32,(B,B),0); ri=lax.broadcasted_iota(jnp.int32,(B,B),1)
                ss=[jnp.where(ki<=ri,v,-1e30) for v in ss]
            mo=[ms[h] for h in H]
            mn=[jnp.maximum(mo[h],jnp.max(ss[h],axis=0,keepdims=True)) for h in H]
            al=[jnp.exp(mo[h]-mn[h]) for h in H]
            pp=[jnp.exp(ss[h]-mn[h]) for h in H]
            for h in H: ls[h]=ls[h]*al[h]+jnp.sum(pp[h],axis=0,keepdims=True)
            pb=[v.astype(bf) for v in pp]
            for h in H:
                ps[h,kb]=pb[h]
                mk[h,kb]=mn[h]
                ms[h]=mn[h]
            ob=[dg(kvt[kb,64:,:],pb[h],NN) for h in H]
            for h in H: ots[h]=ots[h]*al[h]+ob[h]
        def fstep(kb,carry):
            @pl.when(kb<rb)
            def _(): fwd(kb,False)
            @pl.when(kb==rb)
            def _(): fwd(kb,True)
            between(pair,kb,0)
            return carry
        lax.fori_loop(0,nkb,fstep,0)
        dot_=do.astype(f32).T
        for h in range(2):
            inv=1.0/ls[h]
            ot=ots[h]*inv
            ots[h]=ot
            ls[h]=inv
        delta=[jnp.sum(ots[h]*dot_[64*h:64*h+64,:],axis=0,keepdims=True) for h in range(2)]
        o_ref[own,cols]=jnp.concatenate([ots[0],ots[1]],axis=0).T.astype(bf)
        def bwd(kb):
            dps=[dg(v2[kb],dom[h],NT) for h in H]
            al=[jnp.exp(mk[h,kb]-ms[h])*ls[h] for h in H]
            pp=[ps[h,kb].astype(f32)*al[h] for h in H]
            ds=[(pp[h]*(dps[h]-delta[h])).astype(bf) for h in H]
            pn=[v.astype(bf) for v in pp]
            acck[kb]+=dg(ds[0],qm[0],NN)+dg(ds[1],qm[1],NN)
            accv[kb]+=dg(pn[0],dom[0],NN)+dg(pn[1],dom[1],NN)
            qb=[dg(kvt[kb,:64,:],ds[h],NN) for h in H]
            for h in H: dqs[h]+=qb[h]
        def bstep(kb,carry):
            @pl.when(kb<=rb)
            def _(): bwd(kb)
            between(pair,kb,1)
            return carry
        lax.fori_loop(0,nkb,bstep,0)
        dq_ref[own,cols]=(turn(jnp.concatenate([dqs[0],dqs[1]],axis=0).T,cos_ref[...],sin_ref[...],True)*HD**-0.5).astype(bf)
        return carry
    lax.fori_loop(0,pairs,one,0)
    def flush(kb,carry):
        k=acck[kb]; v=accv[kb]
        k=jnp.where(lane,k+pltpu.roll(k,64,1),v+pltpu.roll(v,64,1))
        if join: dkvs[kb]=k
        else: dkv_ref[0,pl.ds(pl.multiple_of(kb*B,B),B),:]=k
        return carry
    lax.fori_loop(0,nkb,flush,0)
    if join:
        sums.one(1,part1)
        sums.two(1,part1)
    if comm: end()
    if join:
        sums.three(1,part1)
        for cp in before: cp.wait()

def attention(b,q,do,kv,cos,sin,comm,arrays,dp,cid,prev=()):
    S=kv.shape[1]; nkb=S//B; width=q.shape[1]; join=len(prev)>0
    assert not join or (b==1 and nkb==4)
    whole=lambda *shape: pl.BlockSpec(shape,lambda *_: (0,)*len(shape))
    blk=pl.BlockSpec((B,width),lambda *_: (b,0))
    kvs=pl.BlockSpec((1,S,128),lambda *_: (b,0,0))
    hbm=pl.BlockSpec(memory_space=pl.ANY)
    rows=2*B if join else B
    outs=[jax.ShapeDtypeStruct((rows,width),bf),jax.ShapeDtypeStruct((rows,width+128*join),bf)]+([] if join else [jax.ShapeDtypeStruct((1,S,128),f32)])
    params=dict(vmem_limit_bytes=62<<20)
    if comm: params.update(collective_id=cid,has_side_effects=True)
    return pl.pallas_call(functools.partial(attn_kernel,dp//2,width//128,comm,join,len(arrays)),
      grid_spec=pltpu.PrefetchScalarGridSpec(num_scalar_prefetch=0,grid=(1,),
        in_specs=[blk,blk,kvs,whole(B,128),whole(B,128)]+([hbm,hbm,whole(1,S,128)] if join else [])+(comm.ins if comm else []),
        out_specs=[whole(*t.shape) for t in outs]+(comm.outs if comm else []),
        scratch_shapes=[pltpu.VMEM((nkb,B,128),bf),pltpu.VMEM((nkb,B,128),bf),pltpu.VMEM((nkb,128,B),bf),pltpu.VMEM((nkb,B,128),f32),pltpu.VMEM((nkb,B,128),f32),
                        pltpu.VMEM((2,nkb,B,B),bf),pltpu.VMEM((2,nkb,1,B),f32),pltpu.VMEM((2,1,B),f32),pltpu.VMEM((2,1,B),f32),pltpu.VMEM((2,64,B),f32),pltpu.VMEM((2,64,B),f32)]
                       +([pltpu.VMEM((nkb,B,128),f32),pltpu.SemaphoreType.DMA((2,))]+Fold.scratch if join else [])
                       +(comm.scratch if comm else [])),
      out_shape=outs+(comm.shapes if comm else []),
      compiler_params=pltpu.CompilerParams(**params),name="attn")(q,do,kv,cos,sin,*prev,*arrays)


def kv_gather_kernel(nz, own_ref, full_ref, send, recv):
    pos = coords(nz)
    z, x, y, c = pos
    greet(pos, ["y", "c"], nz)
    nb = own_ref.shape[0]
    sent = []

    def go(b, m, src, kind):
        cp = pltpu.make_async_remote_copy(src, full_ref.at[b, m], send.at[len(sent)], recv.at[b, m],
                                          device_id=peer(pos, kind, nz), device_id_type=MESH)
        cp.start()
        sent.append(cp)

    def wait(b, m):
        pltpu.make_async_remote_copy(full_ref.at[b, m], full_ref.at[b, m], send.at[0], recv.at[b, m],
                                     device_id=peer(pos, "c", nz), device_id_type=MESH).wait_recv()

    for b in range(nb):
        go(b, y * 2 + c, own_ref.at[b], "y")
    for b in range(nb):
        go(b, y * 2 + c, own_ref.at[b], "c")
    for b in range(nb):
        full_ref[b, y * 2 + c] = own_ref[b]
    for b in range(nb):
        m = (1 - y) * 2 + c
        wait(b, m)
        go(b, m, full_ref.at[b, m], "c")
    for b in range(nb):
        wait(b, y * 2 + 1 - c)
        wait(b, (1 - y) * 2 + 1 - c)
    for cp in sent:
        cp.wait_send()


def kv_gather(own, dp, cid):
    nb, rows, w = own.shape
    return pl.pallas_call(
        functools.partial(kv_gather_kernel, dp // 2),
        in_specs=[pl.BlockSpec(memory_space=pltpu.VMEM)],
        out_specs=pl.BlockSpec(memory_space=pltpu.VMEM),
        out_shape=jax.ShapeDtypeStruct((nb, 4, rows, w), own.dtype),
        scratch_shapes=[pltpu.SemaphoreType.DMA((3 * nb,)), pltpu.SemaphoreType.DMA((nb, 4))],
        compiler_params=pltpu.CompilerParams(collective_id=cid, has_side_effects=True),
        name="gather_keyval",
    )(own)


def kv_reduce_kernel(nz, n, *refs):
    parts = refs[:n]
    cos_ref, sin_ref, out_ref, low, cbuf, ybuf, ysend, send, crecv, yrecv = refs[n:]
    pos = coords(nz)
    z, x, y, c = pos
    greet(pos, ["y", "c"], nz)
    sent = []

    def go(src, dst, sem, kind):
        cp = pltpu.make_async_remote_copy(src, dst, send.at[len(sent)], sem, device_id=peer(pos, kind, nz), device_id_type=MESH)
        cp.start()
        sent.append(cp)

    def wait(dst, sem):
        pltpu.make_async_remote_copy(dst, dst, send.at[0], sem, device_id=peer(pos, "c", nz), device_id_type=MESH).wait_recv()

    for ry in (1, 0):
        yy = 1 - y if ry else y
        for b in range(n):
            low[b, ry] = parts[b][yy * 2 + 1 - c].astype(bf)
            go(low.at[b, ry], cbuf.at[b, ry], crecv.at[b, ry], "c")
    for b in range(n):
        wait(cbuf.at[b, 1], crecv.at[b, 1])
        ysend[b] = (parts[b][(1 - y) * 2 + c] + cbuf[b, 1].astype(f32)).astype(bf)
        go(ysend.at[b], ybuf.at[b], yrecv.at[b], "y")
    for b in range(n):
        wait(cbuf.at[b, 0], crecv.at[b, 0])
        wait(ybuf.at[b], yrecv.at[b])
        v = parts[b][y * 2 + c] + cbuf[b, 0].astype(f32) + ybuf[b].astype(f32)
        out_ref[b] = turn(v, cos_ref[...], sin_ref[...], True, True).astype(bf)
    for cp in sent:
        cp.wait_send()


def kv_reduce(parts, cos, sin, dp, cid):
    nb = len(parts)
    mp, rows, w = parts[0].shape
    vm = pl.BlockSpec(memory_space=pltpu.VMEM)
    return pl.pallas_call(
        functools.partial(kv_reduce_kernel, dp // 2, nb),
        in_specs=[vm] * (nb + 2),
        out_specs=vm,
        out_shape=jax.ShapeDtypeStruct((nb, rows, w), bf),
        scratch_shapes=[pltpu.VMEM((nb, 2, rows, w), bf), pltpu.VMEM((nb, 2, rows, w), bf), pltpu.VMEM((nb, rows, w), bf),
                        pltpu.VMEM((nb, rows, w), bf), pltpu.SemaphoreType.DMA((3 * nb,)), pltpu.SemaphoreType.DMA((nb, 2)), pltpu.SemaphoreType.DMA((nb,))],
        compiler_params=pltpu.CompilerParams(collective_id=cid, has_side_effects=True),
        name="reduce_keyval",
    )(*parts, cos, sin)


def spread(arrays, inside, dp, mp):
    out = []
    for i, s in enumerate(arrays):
        if i in inside:
            out.append(lax.all_gather(s, "dp"))
        else:
            a = lax.all_gather(s, ("dp", "mp")).reshape((dp, mp) + s.shape)
            out.append(a.transpose(0, 2, 1, 3).reshape(dp, s.shape[0], -1))
    return out


def collect(parts, inside, dp, mp):
    out = []
    for i, p in enumerate(parts):
        p = p.astype(f32)
        if i in inside:
            out.append(lax.psum(lax.psum_scatter(p, "dp", scatter_dimension=0), "mp"))
        else:
            a = p.reshape(dp, p.shape[1], mp, -1).transpose(0, 2, 1, 3).reshape(dp * mp, p.shape[1], -1)
            out.append(lax.psum_scatter(a, ("dp", "mp"), scatter_dimension=0))
    return out


def rotary(position):
    lane = jnp.arange(2 * HD, dtype=jnp.int32)
    inside = lane % HD
    frequency = 10000.0 ** (-2.0 * (inside % (ROT // 2)).astype(f32) / ROT)
    angle = position[:, None].astype(f32) * frequency[None, :]
    turned = (inside < ROT)[None, :]
    return jnp.where(turned, jnp.cos(angle), 1.0), jnp.where(turned, jnp.sin(angle), 0.0)


def plain_prologue(tokens, cos, sin, wq, wo, wkv, gains, biases, dp, mp):
    nb, own, width = tokens.shape
    wq, wo, kvg = spread([wq, wo, jnp.concatenate([wkv, gains, biases], axis=1)], {2}, dp, mp)
    kvg = kvg.reshape(width, -1)
    small = kvg[:, 2 * HD :].astype(f32).T
    x = tokens.reshape(nb * own, width).astype(f32)
    centered = x - jnp.mean(x, axis=1, keepdims=True)
    normed = centered * lax.rsqrt(jnp.mean(centered * centered, axis=1, keepdims=True) + epsilon)
    ain = (normed * small[0] + small[2]).astype(bf)
    mlp_in = (normed * small[1] + small[3]).astype(bf)
    kv = jnp.dot(ain, kvg[:, : 2 * HD], preferred_element_type=f32).reshape(nb, own, 2 * HD)
    first, half = jnp.arange(2 * HD) < HD, ROT // 2
    other = jnp.where(jnp.arange(2 * HD) < half, -jnp.roll(kv, -half, axis=2), jnp.roll(kv, half, axis=2)) * sin
    kv = jnp.where(first, kv * cos + other, kv).astype(bf)
    return wq, wo, jnp.concatenate([small, small]), normed, ain, mlp_in, kv_gather(kv, dp, 3), jnp.concatenate([wq.reshape(width, width), kvg[:, : 2 * HD]], axis=1)


def shards(tokens, norm_gains, norm_biases, w_query, w_keyval, w_output, w_up, w_down, cotangent, subset_ids, subset_weights):
    dp, mp = lax.axis_size("dp"), lax.axis_size("mp")
    me = lax.axis_index("mp")
    nb, own, width = tokens.shape
    rows = nb * own
    part, cols = w_query.shape
    ff = w_up.shape[1]
    mine = dp == 8
    dot = functools.partial(jnp.dot, preferred_element_type=f32)
    nt = lambda a, b: lax.dot_general(a, b, (((1,), (1,)), ((), ())), preferred_element_type=f32)
    tn = lambda a, b: lax.dot_general(a, b, (((0,), (0,)), ((), ())), preferred_element_type=f32)
    cos, sin = rotary(me * own + jnp.arange(own, dtype=jnp.int32))
    small_weights = (w_query, w_output, w_keyval, norm_gains, norm_biases)
    if mine:
        wq, wo, small, normed, attn_in, mlp_in, kv, wqkv = prologue(tokens, cos, sin, *small_weights, dp, mp, 1)
    else:
        wq, wo, small, normed, attn_in, mlp_in, kv, wqkv = plain_prologue(tokens, cos, sin, *small_weights, dp, mp)
    wq, wo, wqkv = wq.reshape(width, width), wo.reshape(width, width), wqkv.reshape(width, -1)
    kv_full = kv.reshape(nb, mp * own, 2 * HD)
    gain_a, gain_m = small[0], small[1]

    ids = lax.dynamic_slice_in_dim(subset_ids.reshape(nb, mp * own), me * own, own, 1).reshape(rows)
    matches = ids[:, None] == jnp.arange(subset_weights.shape[0], dtype=jnp.int32)[None, :]
    scale = jnp.sum(jnp.where(matches, subset_weights[None, :], 0.0), axis=1, keepdims=True)
    g = (cotangent.reshape(rows, width).astype(f32) * scale).astype(bf)

    q = dot(attn_in, wq)
    grad_heads = dot(g, wo).astype(bf)
    mlp_plan = lambda a, b: [(0, 0, 768, a), (1, 0, 256, a), (1, 256, 768, b)]
    if mine:
        o0, dq0, dkv0, up, down = attention(0, q, grad_heads, kv_full, cos, sin, Gather([w_up, w_down], mlp_plan("zyx", "xzy"), dp, mp), [w_up, w_down], dp, 5)
    else:
        o0, dq0, dkv0 = attention(0, q, grad_heads, kv_full, cos, sin, None, [], dp, 5)
        up, down = spread([w_up, w_down], (), dp, mp)
    up = up.reshape(width, mp * ff)
    down = down.reshape(width, mp * ff)

    pre = dot(mlp_in, up)
    cdf = 0.5 * (1.0 + lax.erf(pre * sqrt_half))
    hidden = (pre * cdf).astype(bf)
    slope = (cdf + pre * (jnp.exp(-0.5 * pre * pre) * inv_sqrt_two_pi)).astype(bf)
    hidden, slope = lax.optimization_barrier((hidden, slope))
    dpre = (dot(g, down) * slope).astype(bf)
    gup = tn(mlp_in, dpre).astype(bf).reshape(dp, part, mp * ff)
    gdown = tn(g, hidden).astype(bf).reshape(dp, part, mp * ff)
    if mine:
        o, dqkv, grad_up, grad_down = attention(1, q, grad_heads, kv_full, cos, sin, Scatter([gup, gdown], mlp_plan("xyz", "yzx"), dp, mp), [gup, gdown], dp, 6, (o0, dq0, dkv0))
    else:
        o1, dq1, dkv1 = attention(1, q, grad_heads, kv_full, cos, sin, None, [], dp, 6)
        grad_up, grad_down = collect([gup, gdown], (), dp, mp)
        dkvp = kv_reduce([d.reshape(mp, own, 2 * HD) for d in (dkv0, dkv1)], cos, sin, dp, 4)
        o = jnp.concatenate([o0, o1])
        dqkv = jnp.concatenate([jnp.concatenate([dq0, dq1]), dkvp.reshape(rows, 2 * HD)], axis=1)

    dmlp = nt(dpre, up)
    dattn = nt(dqkv, wqkv)
    dnormed = dattn * gain_a + dmlp * gain_m
    sums = [jnp.sum(dattn * normed, axis=0), jnp.sum(dmlp * normed, axis=0), jnp.sum(dattn, axis=0), jnp.sum(dmlp, axis=0)]
    gq = tn(attn_in, dqkv).astype(bf).reshape(dp, part, -1)
    go = tn(g, o).astype(bf).reshape(dp, part, width)
    k = 2 * HD
    if mine:
        sums = jnp.concatenate([s[None] for s in sums] + [jnp.zeros((4, width), f32)])
        flat = lambda a: a.reshape(rows, width)
        grad_query, grad_output, grad_keyval, gb, out, input_grad = scatter_small(gq, go, sums, o, wo, hidden, down, flat(tokens), flat(cotangent), scale, dnormed, dp, mp, 2)
        grad_gains, grad_biases = gb[:2].T, gb[2:4].T
    else:
        x = tokens.reshape(rows, width).astype(f32)
        out = (x + nt(o, wo) + nt(hidden, down)).astype(bf)
        centered = x - jnp.mean(x, axis=1, keepdims=True)
        inverse = lax.rsqrt(jnp.mean(centered * centered, axis=1, keepdims=True) + epsilon)
        dx = (dnormed - jnp.mean(dnormed, axis=1, keepdims=True) - normed * jnp.mean(dnormed * normed, axis=1, keepdims=True)) * inverse
        input_grad = (cotangent.reshape(rows, width).astype(f32) * scale + dx).astype(bf)
        gq, gkv = gq[:, :, :width], gq[:, :, width:].astype(f32)
        gkvg = jnp.concatenate([gkv, jnp.stack(sums, axis=1).reshape(dp, part, 4)], axis=2)
        grad_query, grad_output, c = collect([gq, go, gkvg], {2}, dp, mp)
        grad_keyval, grad_gains, grad_biases = c[:, :k], c[:, k : k + 2], c[:, k + 2 : k + 4]
    return (
        out.reshape(tokens.shape),
        kv_full.reshape(-1, 2 * HD),
        input_grad.reshape(tokens.shape),
        grad_gains,
        grad_biases,
        grad_query,
        grad_keyval,
        grad_output,
        grad_up,
        grad_down,
    )


def solution(mesh):
    rows = P(None, ("dp", "mp"), None)
    d, dm = P("dp", None), P("dp", "mp")
    return jax.shard_map(
        shards,
        mesh=mesh,
        in_specs=(rows, d, d, dm, d, dm, dm, dm, rows, P("dp"), P()),
        out_specs=(rows, d, rows, d, d, dm, d, dm, dm, dm),
        check_vma=False,
    )
```

profile of v0, /device:TPU:0, one launch (start us, length us, event | category | flops | bytes accessed | tf_op | source)
XLA Modules:
  0.0 305.6 jit_solution(8972887310142599588)
XLA Ops:
  0.7 1.8 fusion.6
  2.5 37.0 %gather_weights.1 = (bf16[8,96,768]{2,1,0:T(8,128)(2,1)}, bf16[8,96,768]{2,1,0:T(8,128)(2,1)}, f32[8,768]{1,0:T(8,128)}, f32[1024,768]{1,0:T(8,128)}, bf16[1024,...) custom-call(bf16[2,512,768]{2,1,0:T(8,128)(2,1)} %refs_0_.1, ...), custom_call_target="tpu_custom_call" | custom-call | tf_op jit(solution)/shard_map/gather_weights/pallas_call | solution.py:442
  39.5 0.0 copy-start.14
  39.5 0.0 copy-start.15
  39.5 5.0 %fusion.12.refs_0_ = f32[1024,768]{1,0:T(8,128)} fusion(bf16[1024,768]{1,0:T(8,128)(2,1)} %get-tuple-element.35, bf16[768,768]{1,0:T(8,128)(2,1)} %bitcast.70), kind=kOutput, calls=%fused_computation.41 | convolution fusion | flops 1207959552 | bytes 5898240 | tf_op jit(solution)/shard_map/dot_general | solution.py:813
  44.6 0.1 select_reduce_fusion
  44.7 0.3 multiply_convert_fusion.3
  45.1 0.8 copy-done.8
  45.8 2.5 convolution_convert_fusion.2.refs_1_
  48.4 67.3 %attn.2 = (bf16[512,768]{1,0:T(8,128)(2,1)}, bf16[512,768]{1,0:T(8,128)(2,1)}, f32[1,2048,128]{2,1,0:T(8,128)}, bf16[8,96,3072]{2,1,0:T(8,128)(2,1)}, bf16[8,96,3072]{2,1,0:T(8,128)(2,1)}) custom-call(f32[1024,768]{1,0:T(8,128)} %fusion.12.refs_0_, bf16[1024,768]{1,0:T(8,128)(2,1)} %convolution_convert_fusion.2.refs_1_, bf16[2,2048,128]{2,1,0:T(8,128)(2,1)} %bitcast.44, ...), custom_call_target="tpu_custom_call" | custom-call | tf_op jit(solution)/shard_map/attn/pallas_call | solution.py:629
  115.7 20.5 %fusion.4 = (bf16[1024,3072]{1,0:T(8,128)(2,1)S(1)}, bf16[1024,3072]{1,0:T(8,128)(2,1)S(1)}) fusion(bf16[1024,768]{1,0:T(8,128)(2,1)} %get-tuple-element.42, bf16[768,3072]{1,0:T(8,128)(2,1)} %bitcast.67), kind=kOutput, calls=%fused_computation.5 | convolution fusion | flops 4866441216 | bytes 18874368 | tf_op jit(solution)/shard_map/dot_general | solution.py:824
  136.3 5.3 %multiply_convert_fusion = bf16[1024,3072]{1,0:T(8,128)(2,1)S(1)} fusion(bf16[1024,3072]{1,0:T(8,128)(2,1)S(1)} %get-tuple-element.45, bf16[1024,768]{1,0:T(8,128)(2,1)S(1)} %bitcast.58, bf16[768,3072]{1,0:T(8,128)(2,1)S(1)} %bitcast.54), kind=kOutput, calls=%fused_computation.6 | convolution fusion | flops 4841275392 | bytes 18874368 | tf_op jit(solution)/shard_map/dot_general | solution.py:829
  141.7 7.0 %convolution_convert_fusion.1 = bf16[768,3072]{1,0:T(8,128)(2,1)} fusion(bf16[1024,768]{1,0:T(8,128)(2,1)S(1)} %copy-done.17, bf16[1024,3072]{1,0:T(8,128)(2,1)S(1)} %multiply_convert_fusion), kind=kOutput, calls=%fused_computation.10 | convolution fusion | flops 4834197504 | bytes 12582912 | tf_op jit(solution)/shard_map/dot_general | solution.py:797
  148.6 7.2 %convolution_convert_fusion = bf16[768,3072]{1,0:T(8,128)(2,1)} fusion(bf16[1024,3072]{1,0:T(8,128)(2,1)S(1)} %get-tuple-element.46.refs_6_, bf16[1024,768]{1,0:T(8,128)(2,1)S(1)} %bitcast.49, f32[1024]{0:T(1024)S(1)} %select_reduce_fusion), kind=kOutput, calls=%fused_computation.9 | convolution fusion | flops 4836556800 | bytes 12587008 | tf_op jit(solution)/shard_map/dot_general | solution.py:797
  155.8 81.6 %attn.3 = (bf16[1024,768]{1,0:T(8,128)(2,1)}, bf16[1024,896]{1,0:T(8,128)(2,1)}, f32[96,768]{1,0:T(8,128)}, f32[96,768]{1,0:T(8,128)}) custom-call(f32[1024,768]{1,0:T(8,128)} %fusion.12.refs_0_, bf16[1024,768]{1,0:T(8,128)(2,1)} %convolution_convert_fusion.2.refs_1_, bf16[2,2048,128]{2,1,0:T(8,128)(2,1)} %bitcast.45, ...), custom_call_target="tpu_custom_call" | custom-call | tf_op jit(solution)/shard_map/attn/pallas_call | solution.py:629
  237.4 3.9 %fusion.13 = f32[1024,768]{1,0:T(8,128)S(1)} fusion(bf16[1024,896]{1,0:T(8,128)(2,1)} %get-tuple-element.47, bf16[768,896]{1,0:T(8,128)(2,1)} %bitcast.69), kind=kOutput, calls=%fused_computation.42 | convolution fusion | flops 1409286144 | bytes 6356992 | tf_op jit(solution)/shard_map/dot_general | solution.py:796
  241.3 0.8 slice_reduce_fusion.1
  242.2 9.6 %fusion.11 = (f32[768]{0:T(1024)S(1)}, f32[768]{0:T(1024)S(1)}, f32[768]{0:T(1024)S(1)}, f32[768]{0:T(1024)S(1)}, f32[1024,768]{1,0:T(8,128)}) fusion(f32[1024,768]{1,0:T(8,128)S(1)} %copy-done.16, f32[1024,768]{1,0:T(8,128)S(1)} %fusion.13, f32[768]{0:T(1024)S(1)} %get-tuple-element.65, f32[768]{0:T(1024)S(1)} %get-tuple-element.64, ...), kind=kOutput, calls=%fused_computation.40 | convolution fusion | flops 4838912000 | bytes 20465664 | tf_op jit(solution)/shard_map/dot_general | solution.py:796
  251.8 0.6 concatenate.3.refs_2_
  252.4 5.0 %convolution_convert_fusion.3 = bf16[768,896]{1,0:T(8,128)(2,1)} fusion(bf16[1024,768]{1,0:T(8,128)(2,1)} %get-tuple-element.35, bf16[1024,896]{1,0:T(8,128)(2,1)} %get-tuple-element.47), kind=kOutput, calls=%fused_computation.17 | convolution fusion | flops 1409974272 | bytes 4784128 | tf_op jit(solution)/shard_map/dot_general | solution.py:797
  257.5 2.6 convolution_convert_fusion.4
  260.1 1.0 copy.22.refs_3_
  261.1 34.5 %scatter_grads.1 = (f32[96,192]{1,0:T(8,128)}, f32[96,192]{1,0:T(8,128)}, f32[96,128]{1,0:T(8,128)}, f32[8,96]{1,0:T(8,128)}, bf16[1024,768]{1,0:T(8,128)(2,1)}, /*index=5*/bf16[1024,768]{1,0:T(8,128)(2,1)}) custom-call(bf16[8,96,896]{2,1,0:T(8,128)(2,1)} %bitcast.59, bf16[8,96,768]{2,1,0:T(8,128)(2,1)} %bitcast.62, f32[8,768]{1,0:T(8,128)} %concatenate.3.refs_2_, ...), custom_call_target="tpu_custom_call" | custom-call | tf_op jit(solution)/shard_map/scatter_grads/pallas_call | solution.py:351
  295.6 1.4 slice_bitcast_fusion
  297.0 2.7 copy.32
  299.7 1.0 copy.33
  300.7 1.1 copy.34
  301.8 0.6 copy.35
  302.5 0.6 copy.36
  303.1 0.6 copy.37
  303.7 0.7 copy.38
  304.4 0.7 copy.39
  (49 shorter events, 0.2 us)
Async XLA Ops:
  39.5 5.1 %copy-start.14 = (s32[4096]{0:T(1024)S(1)}, s32[4096]{0:T(1024)}, u32[]{:S(2)}) copy-start(s32[4096]{0:T(1024)} %param.20) | copy-start | bytes 49156
  39.5 5.1 %copy-start.15 = (f32[22]{0:T(128)S(1)}, f32[22]{0:T(128)}, u32[]{:S(2)}) copy-start(f32[22]{0:T(128)} %param.21) | copy-start | bytes 268
  39.5 5.2 %copy-start.1 = (bf16[2,512,768]{2,1,0:T(8,128)(2,1)S(1)}, bf16[2,512,768]{2,1,0:T(8,128)(2,1)}, u32[]{:S(2)}) copy-start(bf16[2,512,768]{2,1,0:T(8,128)(2,1)} %param.19) | copy-start | bytes 4718596
  44.6 1.3 copy-start.8
  45.1 3.3 %copy-start.6 = (bf16[2,512,768]{2,1,0:T(8,128)(2,1)}, bf16[2,512,768]{2,1,0:T(8,128)(2,1)S(1)}, u32[]{:S(2)}) copy-start(bf16[2,512,768]{2,1,0:T(8,128)(2,1)S(1)} %multiply_convert_fusion.3) | copy-start | bytes 4718596
  115.7 20.6 %copy-start.3 = (bf16[8,96,3072]{2,1,0:T(8,128)(2,1)S(1)}, bf16[8,96,3072]{2,1,0:T(8,128)(2,1)}, u32[]{:S(2)}) copy-start(bf16[8,96,3072]{2,1,0:T(8,128)(2,1)} %get-tuple-element.43) | copy-start | bytes 14155780
  115.7 20.6 %copy-start.7 = (bf16[2,512,768]{2,1,0:T(8,128)(2,1)S(1)}, bf16[2,512,768]{2,1,0:T(8,128)(2,1)}, u32[]{:S(2)}) copy-start(bf16[2,512,768]{2,1,0:T(8,128)(2,1)} %copy-done.6) | copy-start | bytes 4718596
  136.3 12.3 %copy-start.2 = (bf16[1024,3072]{1,0:T(8,128)(2,1)}, bf16[1024,3072]{1,0:T(8,128)(2,1)S(1)}, u32[]{:S(2)}) copy-start(bf16[1024,3072]{1,0:T(8,128)(2,1)S(1)} %get-tuple-element.46.refs_6_) | copy-start | bytes 18874372
  136.3 5.3 %copy-start.17 = (bf16[1024,768]{1,0:T(8,128)(2,1)S(1)}, bf16[1024,768]{1,0:T(8,128)(2,1)}, u32[]{:S(2)}) copy-start(bf16[1024,768]{1,0:T(8,128)(2,1)} %get-tuple-element.42) | copy-start | bytes 4718596
  141.6 7.0 %copy-start.18 = (bf16[1024,3072]{1,0:T(8,128)(2,1)}, bf16[1024,3072]{1,0:T(8,128)(2,1)S(1)}, u32[]{:S(2)}) copy-start(bf16[1024,3072]{1,0:T(8,128)(2,1)S(1)} %multiply_convert_fusion) | copy-start | bytes 18874372
  237.4 4.7 %copy-start.16 = (f32[1024,768]{1,0:T(8,128)S(1)}, f32[1024,768]{1,0:T(8,128)}, u32[]{:S(2)}) copy-start(f32[1024,768]{1,0:T(8,128)} %get-tuple-element.50) | copy-start | bytes 9437188
  237.4 4.7 %copy-start.19 = (bf16[1024,3072]{1,0:T(8,128)(2,1)S(1)}, bf16[1024,3072]{1,0:T(8,128)(2,1)}, u32[]{:S(2)}) copy-start(bf16[1024,3072]{1,0:T(8,128)(2,1)} %copy-done.18) | copy-start | bytes 18874372
  252.4 5.0 %copy-start.4 = (bf16[1024,768]{1,0:T(8,128)(2,1)S(1)}, bf16[1024,768]{1,0:T(8,128)(2,1)}, u32[]{:S(2)}) copy-start(bf16[1024,768]{1,0:T(8,128)(2,1)} %get-tuple-element.48.refs_4_) | copy-start | bytes 4718596
  295.6 4.1 %copy-start = (bf16[2,4,512,128]{3,2,1,0:T(8,128)(2,1)S(1)}, bf16[2,4,512,128]{3,2,1,0:T(8,128)(2,1)}, u32[]{:S(2)}) copy-start(bf16[2,4,512,128]{3,2,1,0:T(8,128)(2,1)} %get-tuple-element.38) | copy-start | bytes 3145732
  295.6 5.1 %copy-start.5 = (bf16[1024,768]{1,0:T(8,128)(2,1)S(1)}, bf16[1024,768]{1,0:T(8,128)(2,1)}, u32[]{:S(2)}) copy-start(bf16[1024,768]{1,0:T(8,128)(2,1)} %get-tuple-element.53) | copy-start | bytes 4718596
  299.7 2.2 copy-start.12
  299.7 2.8 copy-start.13
  299.7 3.4 %copy-start.11 = (f32[96,192]{1,0:T(8,128)S(1)}, f32[96,192]{1,0:T(8,128)}, u32[]{:S(2)}) copy-start(f32[96,192]{1,0:T(8,128)} %get-tuple-element.90) | copy-start | bytes 221188
  299.7 4.1 %copy-start.10 = (f32[96,768]{1,0:T(8,128)S(1)}, f32[96,768]{1,0:T(8,128)}, u32[]{:S(2)}) copy-start(f32[96,768]{1,0:T(8,128)} %get-tuple-element.91) | copy-start | bytes 884740
  299.7 4.8 %copy-start.9 = (f32[96,768]{1,0:T(8,128)S(1)}, f32[96,768]{1,0:T(8,128)}, u32[]{:S(2)}) copy-start(f32[96,768]{1,0:T(8,128)} %get-tuple-element.92) | copy-start | bytes 884740
where the time goes:
time: 308 us; the launch traced here: 306 us
  Pallas kernels  220 us (71%)
  matrix products  68.6 us (22%)
  local copies, waits for them, and re-layouts  12.9 us (4%)
    pallas_call x2, Pallas kernels, attention(): pl.pallas_call(functools.partial(attn_kernel, dp // 2, width // 128, comm...  149 us
    pallas_call x1, Pallas kernels, prologue(): pl.pallas_call(functools.partial(prologue_kernel, dp // 2, comms), in_spe...  37 us
    pallas_call x1, Pallas kernels, scatter_small(): pl.pallas_call(functools.partial(scatter_kernel, comm.nz, comm), in_specs...  34.5 us
    dot_general x4, matrix products, shards(): lax.dot_general(a, b, (((0,), (0,)), ((), ())), preferred_element_type=f32)  21.7 us
    dot_general x1, matrix products, shards(): pre = dot(mlp_in, up)  20.5 us
    dot_general x2, matrix products, shards(): lax.dot_general(a, b, (((1,), (1,)), ((), ())), preferred_element_type=f32)  13.5 us
    unnamed x50, local copies, waits for them, and re-layouts  8.96 us

commit v1 on v0

--- a/solution.py
+++ b/solution.py
@@ -356,16 +356,16 @@
 
 def prologue_kernel(nz,comms,*refs):
     tok_ref,cos_ref,sin_ref,wq_ref,wo_ref,wkv_ref,gain_ref,bias_ref=refs[:8]
-    q_out,o_out,small_out,normed_out,ain_out,min_out,kv_out,all_out=refs[8:16]
-    qo_own,kvg_own,qo_full,kvg_full,wkv_scr,ksend,krecv=refs[16:23]
+    q_out,o_out,small_out,normed_out,aint_out,min_out,kv_out,all_out=refs[8:16]
+    qo_own,kvg_own,qo_full,kvg_full,wkv_scr,ain_out,ksend,krecv=refs[16:24]
     pos=coords(nz); z,x,y,c=pos
     greet(pos,[f"z{k}" for k in range(1,nz)]+["x","y","c"],nz)
     rows=wq_ref.shape[0]
     kvg_own[:,:128]=wkv_ref[...]
     kvg_own[:,128:]=jnp.concatenate([gain_ref[...].astype(f32),bias_ref[...].astype(f32),jnp.zeros((124,rows),f32)],axis=0).T.astype(bf)
     g,b=comms
-    ga=g.build(pos,(kvg_own,),(kvg_full,),refs[23:26])
-    gb=b.build(pos,(qo_own,),(qo_full,),refs[26:29])
+    ga=g.build(pos,(kvg_own,),(kvg_full,),refs[24:27])
+    gb=b.build(pos,(qo_own,),(qo_full,),refs[27:30])
     ga[0]()
     wq=wq_ref[...].astype(f32); wo=wo_ref[...].astype(f32)
     qo_own[:,:128]=wq[:,:128].astype(bf)
@@ -389,7 +389,7 @@
     small=kvg[:,128:].astype(f32).T
     small_out[...]=small[:8]
     wkv=kvg[:,:128]
-    for d in range(q_out.shape[0]): all_out[d,:,width:]=kvg_full[d,:,:128]
+    for d in range(all_out.shape[0]): all_out[d,:,width:]=kvg_full[d,:,:128]
     wkv_scr[...]=wkv
     def copy(s,m,src,kind,n):
         return pltpu.make_async_remote_copy(src,kv_out.at[s,m],ksend.at[n],krecv.at[s,m],device_id=peer(pos,kind,nz),device_id_type=MESH)
@@ -398,7 +398,9 @@
     for s in range(nb):
         def project(k,carry):
             w=pl.ds(pl.multiple_of(k*part,part),part); rows=pl.ds(pl.multiple_of(s*own+k*part,part),part)
-            ain=(normed_out[rows,:]*small[0:1]+small[2:3]).astype(bf)
+            ain=normed_out[rows,:]*small[0:1]+small[2:3]
+            aint_out[:,rows]=ain.T.astype(bf)
+            ain=ain.astype(bf)
             ain_out[rows,:]=ain
             kv_out[s,me,w,:]=turn(dg(ain,wkv_scr[...],NN),cos_ref[w,:],sin_ref[w,:],False,True).astype(bf)
             return carry
@@ -421,14 +423,21 @@
     lane=lax.broadcasted_iota(jnp.int32,(rows,128),1)<64
     def unpack(d,carry):
         def tile(m,k): return qo_full[d,:,384*m+128*k:384*m+128*k+128].astype(f32)
-        for ref,place in ((q_out,[(0,0),(0,1),(1,0)]),(o_out,[(1,1),(2,0),(2,1)])):
-            for j in range(ref.shape[2]//128):
+        for ref,place in ((all_out,[(0,0),(0,1),(1,0)]),(o_out,[(1,1),(2,0),(2,1)])):
+            for j in range(width//128):
                 (m0,(k0,h0)),(m1,(k1,h1))=[(h//3,place[h%3]) for h in (2*j,2*j+1)]
                 t=halves(tile(m0,k0),h0,tile(m1,k1),h1,lane).astype(bf)
                 ref[d,:,128*j:128*j+128]=t
-                if ref is q_out: all_out[d,:,128*j:128*j+128]=t
         return carry
-    lax.fori_loop(0,q_out.shape[0],unpack,0)
+    lax.fori_loop(0,all_out.shape[0],unpack,0)
+    def queries(k,carry):
+        T=own//2
+        rows=pl.ds(pl.multiple_of(k*T,T),T); w=pl.ds(pl.multiple_of(k%2*T,T),T)
+        v=dg(ain_out[rows,:],all_out[:,:,:width].reshape(width,width),NN)
+        for j in range(width//128):
+            q_out[rows,128*j:128*j+128]=(turn(v[:,128*j:128*j+128],cos_ref[w,:],sin_ref[w,:],False)*HD**-0.5).astype(bf)
+        return carry
+    lax.fori_loop(0,2*nb,queries,0)
     for s in range(nb):
         for m in (y*2+1-c,(1-y)*2+1-c): copy(s,m,kv_out.at[s,m],"c",0).wait_recv()
     for cp in copies: cp.wait_send()
@@ -441,8 +450,8 @@
     s=lambda *a: jax.ShapeDtypeStruct(a,bf)
     return pl.pallas_call(functools.partial(prologue_kernel,dp//2,comms),
         in_specs=[vm]*8,out_specs=[vm]*8,
-        out_shape=[s(dp,part,width),s(dp,part,width),jax.ShapeDtypeStruct((8,width),f32),jax.ShapeDtypeStruct((nb*own,width),f32),s(nb*own,width),s(nb*own,width),s(nb,mp,own,128),s(dp,part,width+128)],
-        scratch_shapes=[pltpu.VMEM(qo.shape,bf),pltpu.VMEM(kvg.shape,bf),pltpu.VMEM((dp,part,mp*2*cols),bf),pltpu.VMEM((dp,part,256),bf),pltpu.VMEM((width,128),bf),
+        out_shape=[s(nb*own,width),s(dp,part,width),jax.ShapeDtypeStruct((8,width),f32),jax.ShapeDtypeStruct((nb*own,width),f32),s(width,nb*own),s(nb*own,width),s(nb,mp,own,128),s(dp,part,width+128)],
+        scratch_shapes=[pltpu.VMEM(qo.shape,bf),pltpu.VMEM(kvg.shape,bf),pltpu.VMEM((dp,part,mp*2*cols),bf),pltpu.VMEM((dp,part,256),bf),pltpu.VMEM((width,128),bf),pltpu.VMEM((nb*own,width),bf),
                         pltpu.SemaphoreType.DMA((3*nb,)),pltpu.SemaphoreType.DMA((nb,mp))]+comms[0].scratch+comms[1].scratch,
         compiler_params=pltpu.CompilerParams(collective_id=cid,has_side_effects=True,vmem_limit_bytes=60<<20),name="gather_weights")(tokens,cos,sin,wq,wo,wkv,gains.T,biases.T)
 
@@ -541,7 +550,7 @@
     lax.fori_loop(0,nkb,setup,0)
     def one(pair,carry):
         cols=pl.ds(pl.multiple_of(pair*128,128),128)
-        q=(turn(q_ref[:,cols],cos_ref[...],sin_ref[...],False)*HD**-0.5).astype(bf); do=do_ref[:,cols]
+        q=q_ref[:,cols]; do=do_ref[:,cols]
         zero=jnp.zeros_like(q)
         qm=(jnp.where(lane,q,zero),jnp.where(lane,zero,q))
         dom=(jnp.where(lane,do,zero),jnp.where(lane,zero,do))
@@ -781,7 +790,12 @@
     first, half = jnp.arange(2 * HD) < HD, ROT // 2
     other = jnp.where(jnp.arange(2 * HD) < half, -jnp.roll(kv, -half, axis=2), jnp.roll(kv, half, axis=2)) * sin
     kv = jnp.where(first, kv * cos + other, kv).astype(bf)
-    return wq, wo, jnp.concatenate([small, small]), normed, ain, mlp_in, kv_gather(kv, dp, 3), jnp.concatenate([wq.reshape(width, width), kvg[:, : 2 * HD]], axis=1)
+    wq = wq.reshape(width, width)
+    q = jnp.dot(ain, wq, preferred_element_type=f32).reshape(nb, own, width // 128, 128)
+    low = jnp.arange(128) % HD < half
+    other = jnp.where(low, -jnp.roll(q, -half, axis=3), jnp.roll(q, half, axis=3)) * sin[:, None, :]
+    q = ((q * cos[:, None, :] + other) * HD**-0.5).astype(bf).reshape(nb * own, width)
+    return q, wo, jnp.concatenate([small, small]), normed, ain.T, mlp_in, kv_gather(kv, dp, 3), jnp.concatenate([wq, kvg[:, : 2 * HD]], axis=1)
 
 
 def shards(tokens, norm_gains, norm_biases, w_query, w_keyval, w_output, w_up, w_down, cotangent, subset_ids, subset_weights):
@@ -798,10 +812,10 @@
     cos, sin = rotary(me * own + jnp.arange(own, dtype=jnp.int32))
     small_weights = (w_query, w_output, w_keyval, norm_gains, norm_biases)
     if mine:
-        wq, wo, small, normed, attn_in, mlp_in, kv, wqkv = prologue(tokens, cos, sin, *small_weights, dp, mp, 1)
+        q, wo, small, normed, attn_in_t, mlp_in, kv, wqkv = prologue(tokens, cos, sin, *small_weights, dp, mp, 1)
     else:
-        wq, wo, small, normed, attn_in, mlp_in, kv, wqkv = plain_prologue(tokens, cos, sin, *small_weights, dp, mp)
-    wq, wo, wqkv = wq.reshape(width, width), wo.reshape(width, width), wqkv.reshape(width, -1)
+        q, wo, small, normed, attn_in_t, mlp_in, kv, wqkv = plain_prologue(tokens, cos, sin, *small_weights, dp, mp)
+    wo, wqkv = wo.reshape(width, width), wqkv.reshape(width, -1)
     kv_full = kv.reshape(nb, mp * own, 2 * HD)
     gain_a, gain_m = small[0], small[1]
 
@@ -810,7 +824,6 @@
     scale = jnp.sum(jnp.where(matches, subset_weights[None, :], 0.0), axis=1, keepdims=True)
     g = (cotangent.reshape(rows, width).astype(f32) * scale).astype(bf)
 
-    q = dot(attn_in, wq)
     grad_heads = dot(g, wo).astype(bf)
     mlp_plan = lambda a, b: [(0, 0, 768, a), (1, 0, 256, a), (1, 256, 768, b)]
     if mine:
@@ -842,7 +855,7 @@
     dattn = nt(dqkv, wqkv)
     dnormed = dattn * gain_a + dmlp * gain_m
     sums = [jnp.sum(dattn * normed, axis=0), jnp.sum(dmlp * normed, axis=0), jnp.sum(dattn, axis=0), jnp.sum(dmlp, axis=0)]
-    gq = tn(attn_in, dqkv).astype(bf).reshape(dp, part, -1)
+    gq = dot(attn_in_t, dqkv).astype(bf).reshape(dp, part, -1)
     go = tn(g, o).astype(bf).reshape(dp, part, width)
     k = 2 * HD
     if mine:

time: 308 us -> 305 us (level)
  matrix products: 68.6 us -> 53.5 us
  Pallas kernels: 220 us -> 231 us
    dot_general x1, matrix products: 20.5 us -> 10.2 us  [shards(): pre = dot(mlp_in, up)]
    pallas_call x2, Pallas kernels: 149 us -> 156 us  [attention(): pl.pallas_call(functools.partial(attn_kernel, dp // 2, width // 128, comm...]
    dot_general x4 -> x3, matrix products: 21.7 us -> 16.7 us  [shards(): lax.dot_general(a, b, (((0,), (0,)), ((), ())), preferred_element_type=f32)]
    pallas_call x1, Pallas kernels: 37 us -> 40.3 us  [prologue(): pl.pallas_call(functools.partial(prologue_kernel, dp // 2, comms), in_spe...]
    unnamed x50 -> x46, local copies, waits for them, and re-layouts: 8.96 us -> 8.19 us
where the time goes in v1:
time: 305 us; the launch traced here: 301 us
  Pallas kernels  231 us (76%)
  matrix products  53.5 us (18%)
  local copies, waits for them, and re-layouts  12.9 us (4%)
    pallas_call x2, Pallas kernels, attention(): pl.pallas_call(functools.partial(attn_kernel, dp // 2, width // 128, comm...  156 us
    pallas_call x1, Pallas kernels, prologue(): pl.pallas_call(functools.partial(prologue_kernel, dp // 2, comms), in_spe...  40.3 us
    pallas_call x1, Pallas kernels, scatter_small(): pl.pallas_call(functools.partial(scatter_kernel, comm.nz, comm), in_specs...  34.5 us
    dot_general x3, matrix products, shards(): lax.dot_general(a, b, (((0,), (0,)), ((), ())), preferred_element_type=f32)  16.7 us
    dot_general x2, matrix products, shards(): lax.dot_general(a, b, (((1,), (1,)), ((), ())), preferred_element_type=f32)  13.6 us
    dot_general x1, matrix products, shards(): pre = dot(mlp_in, up)  10.2 us
    unnamed x46, local copies, waits for them, and re-layouts  8.19 us

profile of v1, /device:TPU:0, one launch (start us, length us, event | category | flops | bytes accessed | tf_op | source)
XLA Modules:
  0.0 301.1 jit_solution(7687352898651828361)
XLA Ops:
  0.6 0.0 copy-start.1
  0.7 1.8 fusion.6
  2.5 40.3 %gather_weights.1 = (bf16[1024,768]{1,0:T(8,128)(2,1)}, bf16[8,96,768]{2,1,0:T(8,128)(2,1)}, f32[8,768]{1,0:T(8,128)}, f32[1024,768]{1,0:T(8,128)}, bf16[768,102...) custom-call(bf16[2,512,768]{2,1,0:T(8,128)(2,1)} %refs_0_.1, ...), custom_call_target="tpu_custom_call" | custom-call | tf_op jit(solution)/shard_map/gather_weights/pallas_call | solution.py:451
  42.9 0.8 reshape.109
  43.7 0.7 select_reduce_fusion
  44.5 0.3 multiply_convert_fusion.3
  44.8 0.0 copy-start.6
  44.8 2.5 convolution_convert_fusion.2.refs_1_
  47.4 66.1 %attn.2 = (bf16[512,768]{1,0:T(8,128)(2,1)}, bf16[512,768]{1,0:T(8,128)(2,1)}, f32[1,2048,128]{2,1,0:T(8,128)}, bf16[8,96,3072]{2,1,0:T(8,128)(2,1)}, bf16[8,96,3072]{2,1,0:T(8,128)(2,1)}) custom-call(bf16[1024,768]{1,0:T(8,128)(2,1)} %get-tuple-element.36.refs_0_, bf16[1024,768]{1,0:T(8,128)(2,1)} %convolution_convert_fusion.2.refs_1_, ...), custom_call_target="tpu_custom_call" | custom-call | tf_op jit(solution)/shard_map/attn/pallas_call | solution.py:638
  113.5 0.0 copy-start.7
  113.6 10.2 %fusion.4 = (bf16[1024,3072]{1,0:T(8,128)(2,1)S(1)}, bf16[1024,3072]{1,0:T(8,128)(2,1)S(1)}) fusion(bf16[1024,768]{1,0:T(8,128)(2,1)} %get-tuple-element.42, bf16[768,3072]{1,0:T(8,128)(2,1)} %bitcast.64), kind=kOutput, calls=%fused_computation.5 | convolution fusion | flops 4866441216 | bytes 18874368 | tf_op jit(solution)/shard_map/dot_general | solution.py:837
  123.9 5.6 %multiply_convert_fusion = bf16[1024,3072]{1,0:T(8,128)(2,1)S(1)} fusion(bf16[1024,3072]{1,0:T(8,128)(2,1)S(1)} %get-tuple-element.45, bf16[1024,768]{1,0:T(8,128)(2,1)S(1)} %bitcast.55, bf16[768,3072]{1,0:T(8,128)(2,1)S(1)} %bitcast.49), kind=kOutput, calls=%fused_computation.6 | convolution fusion | flops 4841275392 | bytes 18874368 | tf_op jit(solution)/shard_map/dot_general | solution.py:842
  129.5 6.9 %convolution_convert_fusion.1 = bf16[768,3072]{1,0:T(8,128)(2,1)} fusion(bf16[1024,768]{1,0:T(8,128)(2,1)S(1)} %copy-done.15, bf16[1024,3072]{1,0:T(8,128)(2,1)S(1)} %multiply_convert_fusion), kind=kOutput, calls=%fused_computation.10 | convolution fusion | flops 4834197504 | bytes 12582912 | tf_op jit(solution)/shard_map/dot_general | solution.py:811
  136.4 7.1 %convolution_convert_fusion = bf16[768,3072]{1,0:T(8,128)(2,1)} fusion(bf16[1024,3072]{1,0:T(8,128)(2,1)S(1)} %get-tuple-element.46.refs_6_, bf16[1024,768]{1,0:T(8,128)(2,1)S(1)} %bitcast.46, f32[1024]{0:T(1024)S(1)} %select_reduce_fusion), kind=kOutput, calls=%fused_computation.9 | convolution fusion | flops 4836556800 | bytes 12587008 | tf_op jit(solution)/shard_map/dot_general | solution.py:811
  143.5 89.6 %attn.3 = (bf16[1024,768]{1,0:T(8,128)(2,1)}, bf16[1024,896]{1,0:T(8,128)(2,1)}, f32[96,768]{1,0:T(8,128)}, f32[96,768]{1,0:T(8,128)}) custom-call(bf16[1024,768]{1,0:T(8,128)(2,1)} %get-tuple-element.36.refs_0_, bf16[1024,768]{1,0:T(8,128)(2,1)} %convolution_convert_fusion.2.refs_1_, bf16[2,2048,128]{2,1,0:T(8,128)(2,1)} %bitcast.42, ...), custom_call_target="tpu_custom_call" | custom-call | tf_op jit(solution)/shard_map/attn/pallas_call | solution.py:638
  233.2 3.9 %fusion.12 = f32[1024,768]{1,0:T(8,128)S(1)} fusion(bf16[1024,896]{1,0:T(8,128)(2,1)} %get-tuple-element.47, bf16[768,896]{1,0:T(8,128)(2,1)} %bitcast.66), kind=kOutput, calls=%fused_computation.41 | convolution fusion | flops 1409286144 | bytes 6356992 | tf_op jit(solution)/shard_map/dot_general | solution.py:810
  237.0 0.8 slice_reduce_fusion.1
  237.9 9.7 %fusion.11 = (f32[768]{0:T(1024)S(1)}, f32[768]{0:T(1024)S(1)}, f32[768]{0:T(1024)S(1)}, f32[768]{0:T(1024)S(1)}, f32[1024,768]{1,0:T(8,128)}) fusion(f32[1024,768]{1,0:T(8,128)S(1)} %copy-done.14, f32[1024,768]{1,0:T(8,128)S(1)} %fusion.12, f32[768]{0:T(1024)S(1)} %get-tuple-element.65, f32[768]{0:T(1024)S(1)} %get-tuple-element.64, ...), kind=kOutput, calls=%fused_computation.40 | convolution fusion | flops 4838912000 | bytes 20465664 | tf_op jit(solution)/shard_map/dot_general | solution.py:810
  247.6 0.6 concatenate.3.refs_2_
  248.2 5.0 %convolution_convert_fusion.3 = bf16[768,896]{1,0:T(8,128)(2,1)} fusion(bf16[768,1024]{1,0:T(8,128)(2,1)} %get-tuple-element.35, bf16[1024,896]{1,0:T(8,128)(2,1)} %get-tuple-element.47), kind=kOutput, calls=%fused_computation.17 | convolution fusion | flops 1409974272 | bytes 4784128 | tf_op jit(solution)/shard_map/dot_general | solution.py:858
  253.2 2.6 convolution_convert_fusion.4
  255.8 1.0 copy.22.refs_3_
  256.9 34.5 %scatter_grads.1 = (f32[96,192]{1,0:T(8,128)}, f32[96,192]{1,0:T(8,128)}, f32[96,128]{1,0:T(8,128)}, f32[8,96]{1,0:T(8,128)}, bf16[1024,768]{1,0:T(8,128)(2,1)}, /*index=5*/bf16[1024,768]{1,0:T(8,128)(2,1)}) custom-call(bf16[8,96,896]{2,1,0:T(8,128)(2,1)} %bitcast.56, bf16[8,96,768]{2,1,0:T(8,128)(2,1)} %bitcast.59, f32[8,768]{1,0:T(8,128)} %concatenate.3.refs_2_, ...), custom_call_target="tpu_custom_call" | custom-call | tf_op jit(solution)/shard_map/scatter_grads/pallas_call | solution.py:351
  291.4 1.4 slice_bitcast_fusion
  292.8 2.7 copy.32
  295.5 1.0 copy.33
  296.4 1.1 copy.34
  297.6 0.6 copy.35
  298.2 0.6 copy.36
  298.8 0.6 copy.37
  299.5 0.7 copy.38
  300.2 0.7 copy.39
  (44 shorter events, 0.1 us)
Async XLA Ops:
  0.6 43.8 %copy-start.1 = (bf16[2,512,768]{2,1,0:T(8,128)(2,1)S(1)}, bf16[2,512,768]{2,1,0:T(8,128)(2,1)}, u32[]{:S(2)}) copy-start(bf16[2,512,768]{2,1,0:T(8,128)(2,1)} %param.19) | copy-start | bytes 4718596
  42.9 2.0 copy-start.8
  44.8 2.6 copy-start.6
  113.5 10.3 %copy-start.3 = (bf16[8,96,3072]{2,1,0:T(8,128)(2,1)S(1)}, bf16[8,96,3072]{2,1,0:T(8,128)(2,1)}, u32[]{:S(2)}) copy-start(bf16[8,96,3072]{2,1,0:T(8,128)(2,1)} %get-tuple-element.43) | copy-start | bytes 14155780
  113.5 10.3 %copy-start.7 = (bf16[2,512,768]{2,1,0:T(8,128)(2,1)S(1)}, bf16[2,512,768]{2,1,0:T(8,128)(2,1)}, u32[]{:S(2)}) copy-start(bf16[2,512,768]{2,1,0:T(8,128)(2,1)} %copy-done.6) | copy-start | bytes 4718596
  123.8 12.5 %copy-start.2 = (bf16[1024,3072]{1,0:T(8,128)(2,1)}, bf16[1024,3072]{1,0:T(8,128)(2,1)S(1)}, u32[]{:S(2)}) copy-start(bf16[1024,3072]{1,0:T(8,128)(2,1)S(1)} %get-tuple-element.46.refs_6_) | copy-start | bytes 18874372
  123.8 5.6 %copy-start.15 = (bf16[1024,768]{1,0:T(8,128)(2,1)S(1)}, bf16[1024,768]{1,0:T(8,128)(2,1)}, u32[]{:S(2)}) copy-start(bf16[1024,768]{1,0:T(8,128)(2,1)} %get-tuple-element.42) | copy-start | bytes 4718596
  129.4 6.9 %copy-start.16 = (bf16[1024,3072]{1,0:T(8,128)(2,1)}, bf16[1024,3072]{1,0:T(8,128)(2,1)S(1)}, u32[]{:S(2)}) copy-start(bf16[1024,3072]{1,0:T(8,128)(2,1)S(1)} %multiply_convert_fusion) | copy-start | bytes 18874372
  233.1 4.7 %copy-start.14 = (f32[1024,768]{1,0:T(8,128)S(1)}, f32[1024,768]{1,0:T(8,128)}, u32[]{:S(2)}) copy-start(f32[1024,768]{1,0:T(8,128)} %get-tuple-element.50) | copy-start | bytes 9437188
  233.1 4.7 %copy-start.17 = (bf16[1024,3072]{1,0:T(8,128)(2,1)S(1)}, bf16[1024,3072]{1,0:T(8,128)(2,1)}, u32[]{:S(2)}) copy-start(bf16[1024,3072]{1,0:T(8,128)(2,1)} %copy-done.16) | copy-start | bytes 18874372
  248.2 5.0 %copy-start.4 = (bf16[1024,768]{1,0:T(8,128)(2,1)S(1)}, bf16[1024,768]{1,0:T(8,128)(2,1)}, u32[]{:S(2)}) copy-start(bf16[1024,768]{1,0:T(8,128)(2,1)} %get-tuple-element.48.refs_4_) | copy-start | bytes 4718596
  291.4 4.1 %copy-start = (bf16[2,4,512,128]{3,2,1,0:T(8,128)(2,1)S(1)}, bf16[2,4,512,128]{3,2,1,0:T(8,128)(2,1)}, u32[]{:S(2)}) copy-start(bf16[2,4,512,128]{3,2,1,0:T(8,128)(2,1)} %get-tuple-element.38) | copy-start | bytes 3145732
  291.4 5.1 %copy-start.5 = (bf16[1024,768]{1,0:T(8,128)(2,1)S(1)}, bf16[1024,768]{1,0:T(8,128)(2,1)}, u32[]{:S(2)}) copy-start(bf16[1024,768]{1,0:T(8,128)(2,1)} %get-tuple-element.53) | copy-start | bytes 4718596
  295.4 2.2 copy-start.12
  295.4 2.8 copy-start.13
  295.4 3.4 %copy-start.11 = (f32[96,192]{1,0:T(8,128)S(1)}, f32[96,192]{1,0:T(8,128)}, u32[]{:S(2)}) copy-start(f32[96,192]{1,0:T(8,128)} %get-tuple-element.90) | copy-start | bytes 221188
  295.4 4.1 %copy-start.10 = (f32[96,768]{1,0:T(8,128)S(1)}, f32[96,768]{1,0:T(8,128)}, u32[]{:S(2)}) copy-start(f32[96,768]{1,0:T(8,128)} %get-tuple-element.91) | copy-start | bytes 884740
  295.4 4.8 %copy-start.9 = (f32[96,768]{1,0:T(8,128)S(1)}, f32[96,768]{1,0:T(8,128)}, u32[]{:S(2)}) copy-start(f32[96,768]{1,0:T(8,128)} %get-tuple-element.92) | copy-start | bytes 884740

commit v2 on v1

--- a/solution.py
+++ b/solution.py
@@ -355,7 +355,8 @@
         compiler_params=pltpu.CompilerParams(collective_id=cid,has_side_effects=True,vmem_limit_bytes=60<<20),name="scatter_grads")(gq,go,sums,scale,*hosted)
 
 def prologue_kernel(nz,comms,*refs):
-    tok_ref,cos_ref,sin_ref,wq_ref,wo_ref,wkv_ref,gain_ref,bias_ref=refs[:8]
+    tok_ref,wq_ref,wo_ref,wkv_ref,gain_ref,bias_ref,cos_ref,sin_ref=refs[:6]+refs[14:16]
+    refs=refs[:2]+refs[:14]+refs[16:]
     q_out,o_out,small_out,normed_out,aint_out,min_out,kv_out,all_out=refs[8:16]
     qo_own,kvg_own,qo_full,kvg_full,wkv_scr,ain_out,ksend,krecv=refs[16:24]
     pos=coords(nz); z,x,y,c=pos
@@ -374,6 +375,14 @@
     gb[0]()
     nb,own,width=tok_ref.shape
     part=own//4
+    half=ROT//2
+    row=lax.broadcasted_iota(jnp.int32,(half,own),0)
+    frequency=jnp.ones((half,own),f32)
+    for i in range(1,half): frequency=jnp.where(row==i,10000.0**(-2.0*i/ROT),frequency)
+    angle=((y*2+c)*own+lax.broadcasted_iota(jnp.int32,(half,own),1)).astype(f32)*frequency
+    for ref,f,rest in ((cos_ref,jnp.cos,jnp.ones),(sin_ref,jnp.sin,jnp.zeros)):
+        t=f(angle); head=[t,t,rest((HD-ROT,own),f32)]
+        ref[...]=jnp.concatenate(head+head,axis=0).T
     def norm(k,carry):
         v=tok_ref[k//4,pl.ds(pl.multiple_of(k%4*part,part),part),:].astype(f32)
         v=v-jnp.mean(v,axis=1,keepdims=True)
@@ -442,18 +451,18 @@
         for m in (y*2+1-c,(1-y)*2+1-c): copy(s,m,kv_out.at[s,m],"c",0).wait_recv()
     for cp in copies: cp.wait_send()
 
-def prologue(tokens,cos,sin,wq,wo,wkv,gains,biases,dp,mp,cid):
+def prologue(tokens,wq,wo,wkv,gains,biases,dp,mp,cid):
     nb,own,width=tokens.shape; part,cols=wq.shape
     kvg=jax.ShapeDtypeStruct((part,256),bf); qo=jax.ShapeDtypeStruct((part,2*cols),bf)
     comms=(Gather([kvg],[(0,0,256,"zx")],dp,mp),Gather([qo],[(0,0,256,"zyx"),(0,256,384,"xzy")],dp,mp))
     vm=pl.BlockSpec(memory_space=pltpu.VMEM)
     s=lambda *a: jax.ShapeDtypeStruct(a,bf)
     return pl.pallas_call(functools.partial(prologue_kernel,dp//2,comms),
-        in_specs=[vm]*8,out_specs=[vm]*8,
-        out_shape=[s(nb*own,width),s(dp,part,width),jax.ShapeDtypeStruct((8,width),f32),jax.ShapeDtypeStruct((nb*own,width),f32),s(width,nb*own),s(nb*own,width),s(nb,mp,own,128),s(dp,part,width+128)],
+        in_specs=[vm]*6,out_specs=[vm]*10,
+        out_shape=[s(nb*own,width),s(dp,part,width),jax.ShapeDtypeStruct((8,width),f32),jax.ShapeDtypeStruct((nb*own,width),f32),s(width,nb*own),s(nb*own,width),s(nb,mp,own,128),s(dp,part,width+128)]+[jax.ShapeDtypeStruct((own,128),f32)]*2,
         scratch_shapes=[pltpu.VMEM(qo.shape,bf),pltpu.VMEM(kvg.shape,bf),pltpu.VMEM((dp,part,mp*2*cols),bf),pltpu.VMEM((dp,part,256),bf),pltpu.VMEM((width,128),bf),pltpu.VMEM((nb*own,width),bf),
                         pltpu.SemaphoreType.DMA((3*nb,)),pltpu.SemaphoreType.DMA((nb,mp))]+comms[0].scratch+comms[1].scratch,
-        compiler_params=pltpu.CompilerParams(collective_id=cid,has_side_effects=True,vmem_limit_bytes=60<<20),name="gather_weights")(tokens,cos,sin,wq,wo,wkv,gains.T,biases.T)
+        compiler_params=pltpu.CompilerParams(collective_id=cid,has_side_effects=True,vmem_limit_bytes=60<<20),name="gather_weights")(tokens,wq,wo,wkv,gains.T,biases.T)
 
 NT=(((1,),(1,)),((),()))
 NN=(((1,),(0,)),((),()))
@@ -809,11 +818,11 @@
     dot = functools.partial(jnp.dot, preferred_element_type=f32)
     nt = lambda a, b: lax.dot_general(a, b, (((1,), (1,)), ((), ())), preferred_element_type=f32)
     tn = lambda a, b: lax.dot_general(a, b, (((0,), (0,)), ((), ())), preferred_element_type=f32)
-    cos, sin = rotary(me * own + jnp.arange(own, dtype=jnp.int32))
     small_weights = (w_query, w_output, w_keyval, norm_gains, norm_biases)
     if mine:
-        q, wo, small, normed, attn_in_t, mlp_in, kv, wqkv = prologue(tokens, cos, sin, *small_weights, dp, mp, 1)
+        q, wo, small, normed, attn_in_t, mlp_in, kv, wqkv, cos, sin = prologue(tokens, *small_weights, dp, mp, 1)
     else:
+        cos, sin = rotary(me * own + jnp.arange(own, dtype=jnp.int32))
         q, wo, small, normed, attn_in_t, mlp_in, kv, wqkv = plain_prologue(tokens, cos, sin, *small_weights, dp, mp)
     wo, wqkv = wo.reshape(width, width), wqkv.reshape(width, -1)
     kv_full = kv.reshape(nb, mp * own, 2 * HD)

time: 305 us -> 305 us (level)
    unnamed x46 -> x42, local copies, waits for them, and re-layouts: 8.19 us -> 8.18 us
where the time goes in v2:
time: 305 us; the launch traced here: 301 us
  Pallas kernels  231 us (76%)
  matrix products  53.6 us (18%)
  local copies, waits for them, and re-layouts  12.9 us (4%)
    pallas_call x2, Pallas kernels, attention(): pl.pallas_call(functools.partial(attn_kernel, dp // 2, width // 128, comm...  156 us
    pallas_call x1, Pallas kernels, prologue(): pl.pallas_call(functools.partial(prologue_kernel, dp // 2, comms), in_spe...  40.3 us
    pallas_call x1, Pallas kernels, scatter_small(): pl.pallas_call(functools.partial(scatter_kernel, comm.nz, comm), in_specs...  34.5 us
    dot_general x3, matrix products, shards(): lax.dot_general(a, b, (((0,), (0,)), ((), ())), preferred_element_type=f32)  16.7 us
    dot_general x2, matrix products, shards(): lax.dot_general(a, b, (((1,), (1,)), ((), ())), preferred_element_type=f32)  13.5 us
    dot_general x1, matrix products, shards(): pre = dot(mlp_in, up)  10.2 us
    unnamed x42, local copies, waits for them, and re-layouts  8.18 us

profile of v2, /device:TPU:0, one launch (start us, length us, event | category | flops | bytes accessed | tf_op | source)
XLA Modules:
  0.0 300.7 jit_solution(2953687696609497242)
XLA Ops:
  0.6 40.3 %gather_weights.1 = (bf16[1024,768]{1,0:T(8,128)(2,1)}, bf16[8,96,768]{2,1,0:T(8,128)(2,1)}, f32[8,768]{1,0:T(8,128)}, f32[1024,768]{1,0:T(8,128)}, bf16[768,102...) custom-call(bf16[2,512,768]{2,1,0:T(8,128)(2,1)} %refs_0_.1, ...), custom_call_target="tpu_custom_call" | custom-call | tf_op jit(solution)/shard_map/gather_weights/pallas_call | solution.py:460
  41.0 0.8 reshape.77
  41.8 0.7 select_reduce_fusion
  42.6 1.7 multiply_convert_fusion.3
  44.3 0.0 copy-done.6
  44.4 2.5 convolution_convert_fusion.2.refs_1_
  46.9 66.2 %attn.2 = (bf16[512,768]{1,0:T(8,128)(2,1)}, bf16[512,768]{1,0:T(8,128)(2,1)}, f32[1,2048,128]{2,1,0:T(8,128)}, bf16[8,96,3072]{2,1,0:T(8,128)(2,1)}, bf16[8,96,3072]{2,1,0:T(8,128)(2,1)}) custom-call(bf16[1024,768]{1,0:T(8,128)(2,1)} %get-tuple-element.38.refs_0_, bf16[1024,768]{1,0:T(8,128)(2,1)} %convolution_convert_fusion.2.refs_1_, ...), custom_call_target="tpu_custom_call" | custom-call | tf_op jit(solution)/shard_map/attn/pallas_call | solution.py:647
  113.1 0.0 copy-start.3
  113.1 10.2 %fusion.4 = (bf16[1024,3072]{1,0:T(8,128)(2,1)S(1)}, bf16[1024,3072]{1,0:T(8,128)(2,1)S(1)}) fusion(bf16[1024,768]{1,0:T(8,128)(2,1)} %get-tuple-element.46, bf16[768,3072]{1,0:T(8,128)(2,1)} %bitcast.64), kind=kOutput, calls=%fused_computation.5 | convolution fusion | flops 4866441216 | bytes 18874368 | tf_op jit(solution)/shard_map/dot_general | solution.py:846
  123.4 5.6 %multiply_convert_fusion = bf16[1024,3072]{1,0:T(8,128)(2,1)S(1)} fusion(bf16[1024,3072]{1,0:T(8,128)(2,1)S(1)} %get-tuple-element.49, bf16[1024,768]{1,0:T(8,128)(2,1)S(1)} %bitcast.55, bf16[768,3072]{1,0:T(8,128)(2,1)S(1)} %bitcast.49), kind=kOutput, calls=%fused_computation.6 | convolution fusion | flops 4841275392 | bytes 18874368 | tf_op jit(solution)/shard_map/dot_general | solution.py:851
  129.0 0.0 copy-start.1
  129.0 6.9 %convolution_convert_fusion.1 = bf16[768,3072]{1,0:T(8,128)(2,1)} fusion(bf16[1024,768]{1,0:T(8,128)(2,1)S(1)} %copy-done.13, bf16[1024,3072]{1,0:T(8,128)(2,1)S(1)} %multiply_convert_fusion), kind=kOutput, calls=%fused_computation.10 | convolution fusion | flops 4834197504 | bytes 12582912 | tf_op jit(solution)/shard_map/dot_general | solution.py:820
  135.9 7.2 %convolution_convert_fusion = bf16[768,3072]{1,0:T(8,128)(2,1)} fusion(bf16[1024,3072]{1,0:T(8,128)(2,1)S(1)} %get-tuple-element.50.refs_6_, bf16[1024,768]{1,0:T(8,128)(2,1)S(1)} %bitcast.46, f32[1024]{0:T(1024)S(1)} %select_reduce_fusion), kind=kOutput, calls=%fused_computation.9 | convolution fusion | flops 4836556800 | bytes 12587008 | tf_op jit(solution)/shard_map/dot_general | solution.py:820
  143.1 89.7 %attn.3 = (bf16[1024,768]{1,0:T(8,128)(2,1)}, bf16[1024,896]{1,0:T(8,128)(2,1)}, f32[96,768]{1,0:T(8,128)}, f32[96,768]{1,0:T(8,128)}) custom-call(bf16[1024,768]{1,0:T(8,128)(2,1)} %get-tuple-element.38.refs_0_, bf16[1024,768]{1,0:T(8,128)(2,1)} %convolution_convert_fusion.2.refs_1_, bf16[2,2048,128]{2,1,0:T(8,128)(2,1)} %bitcast.42, ...), custom_call_target="tpu_custom_call" | custom-call | tf_op jit(solution)/shard_map/attn/pallas_call | solution.py:647
  232.8 3.9 %fusion.6 = f32[1024,768]{1,0:T(8,128)S(1)} fusion(bf16[1024,896]{1,0:T(8,128)(2,1)} %get-tuple-element.51, bf16[768,896]{1,0:T(8,128)(2,1)} %bitcast.66), kind=kOutput, calls=%fused_computation.27 | convolution fusion | flops 1409286144 | bytes 6356992 | tf_op jit(solution)/shard_map/dot_general | solution.py:819
  236.6 0.8 slice_reduce_fusion.1
  237.5 9.7 %fusion.5 = (f32[768]{0:T(1024)S(1)}, f32[768]{0:T(1024)S(1)}, f32[768]{0:T(1024)S(1)}, f32[768]{0:T(1024)S(1)}, f32[1024,768]{1,0:T(8,128)}) fusion(f32[1024,768]{1,0:T(8,128)S(1)} %copy-done.12, f32[1024,768]{1,0:T(8,128)S(1)} %fusion.6, f32[768]{0:T(1024)S(1)} %get-tuple-element.69, f32[768]{0:T(1024)S(1)} %get-tuple-element.68, ...), kind=kOutput, calls=%fused_computation.26 | convolution fusion | flops 4838912000 | bytes 20465664 | tf_op jit(solution)/shard_map/dot_general | solution.py:819
  247.2 0.6 concatenate.3.refs_2_
  247.8 5.0 %convolution_convert_fusion.3 = bf16[768,896]{1,0:T(8,128)(2,1)} fusion(bf16[768,1024]{1,0:T(8,128)(2,1)} %get-tuple-element.37, bf16[1024,896]{1,0:T(8,128)(2,1)} %get-tuple-element.51), kind=kOutput, calls=%fused_computation.17 | convolution fusion | flops 1409974272 | bytes 4784128 | tf_op jit(solution)/shard_map/dot_general | solution.py:867
  252.8 2.7 convolution_convert_fusion.4
  255.5 1.0 copy.22.refs_3_
  256.5 34.5 %scatter_grads.1 = (f32[96,192]{1,0:T(8,128)}, f32[96,192]{1,0:T(8,128)}, f32[96,128]{1,0:T(8,128)}, f32[8,96]{1,0:T(8,128)}, bf16[1024,768]{1,0:T(8,128)(2,1)}, /*index=5*/bf16[1024,768]{1,0:T(8,128)(2,1)}) custom-call(bf16[8,96,896]{2,1,0:T(8,128)(2,1)} %bitcast.56, bf16[8,96,768]{2,1,0:T(8,128)(2,1)} %bitcast.59, f32[8,768]{1,0:T(8,128)} %concatenate.3.refs_2_, ...), custom_call_target="tpu_custom_call" | custom-call | tf_op jit(solution)/shard_map/scatter_grads/pallas_call | solution.py:351
  291.0 1.4 slice_bitcast_fusion
  292.4 2.7 copy.32
  295.1 1.0 copy.33
  296.0 1.1 copy.34
  297.2 0.0 copy-done.10
  297.2 0.6 copy.35
  297.8 0.6 copy.36
  298.4 0.6 copy.37
  299.1 0.7 copy.38
  299.8 0.7 copy.39
  (36 shorter events, 0.1 us)
Async XLA Ops:
  41.0 3.4 %copy-start.6 = (bf16[8,96,768]{2,1,0:T(8,128)(2,1)S(1)}, bf16[8,96,768]{2,1,0:T(8,128)(2,1)}, u32[]{:S(2)}) copy-start(bf16[8,96,768]{2,1,0:T(8,128)(2,1)} %get-tuple-element.39) | copy-start | bytes 3538948
  113.1 10.3 %copy-start.3 = (bf16[8,96,3072]{2,1,0:T(8,128)(2,1)S(1)}, bf16[8,96,3072]{2,1,0:T(8,128)(2,1)}, u32[]{:S(2)}) copy-start(bf16[8,96,3072]{2,1,0:T(8,128)(2,1)} %get-tuple-element.47) | copy-start | bytes 14155780
  123.3 12.5 %copy-start.2 = (bf16[1024,3072]{1,0:T(8,128)(2,1)}, bf16[1024,3072]{1,0:T(8,128)(2,1)S(1)}, u32[]{:S(2)}) copy-start(bf16[1024,3072]{1,0:T(8,128)(2,1)S(1)} %get-tuple-element.50.refs_6_) | copy-start | bytes 18874372
  123.3 5.6 %copy-start.13 = (bf16[1024,768]{1,0:T(8,128)(2,1)S(1)}, bf16[1024,768]{1,0:T(8,128)(2,1)}, u32[]{:S(2)}) copy-start(bf16[1024,768]{1,0:T(8,128)(2,1)} %get-tuple-element.46) | copy-start | bytes 4718596
  128.9 6.9 %copy-start.14 = (bf16[1024,3072]{1,0:T(8,128)(2,1)}, bf16[1024,3072]{1,0:T(8,128)(2,1)S(1)}, u32[]{:S(2)}) copy-start(bf16[1024,3072]{1,0:T(8,128)(2,1)S(1)} %multiply_convert_fusion) | copy-start | bytes 18874372
  129.0 6.9 %copy-start.1 = (bf16[2,512,768]{2,1,0:T(8,128)(2,1)S(1)}, bf16[2,512,768]{2,1,0:T(8,128)(2,1)}, u32[]{:S(2)}) copy-start(bf16[2,512,768]{2,1,0:T(8,128)(2,1)} %param.19) | copy-start | bytes 4718596
  232.7 4.7 %copy-start.12 = (f32[1024,768]{1,0:T(8,128)S(1)}, f32[1024,768]{1,0:T(8,128)}, u32[]{:S(2)}) copy-start(f32[1024,768]{1,0:T(8,128)} %get-tuple-element.54) | copy-start | bytes 9437188
  232.7 4.7 %copy-start.15 = (bf16[1024,3072]{1,0:T(8,128)(2,1)S(1)}, bf16[1024,3072]{1,0:T(8,128)(2,1)}, u32[]{:S(2)}) copy-start(bf16[1024,3072]{1,0:T(8,128)(2,1)} %copy-done.14) | copy-start | bytes 18874372
  247.8 5.0 %copy-start.4 = (bf16[1024,768]{1,0:T(8,128)(2,1)S(1)}, bf16[1024,768]{1,0:T(8,128)(2,1)}, u32[]{:S(2)}) copy-start(bf16[1024,768]{1,0:T(8,128)(2,1)} %get-tuple-element.52.refs_4_) | copy-start | bytes 4718596
  291.0 4.1 %copy-start = (bf16[2,4,512,128]{3,2,1,0:T(8,128)(2,1)S(1)}, bf16[2,4,512,128]{3,2,1,0:T(8,128)(2,1)}, u32[]{:S(2)}) copy-start(bf16[2,4,512,128]{3,2,1,0:T(8,128)(2,1)} %get-tuple-element.40) | copy-start | bytes 3145732
  291.0 5.1 %copy-start.5 = (bf16[1024,768]{1,0:T(8,128)(2,1)S(1)}, bf16[1024,768]{1,0:T(8,128)(2,1)}, u32[]{:S(2)}) copy-start(bf16[1024,768]{1,0:T(8,128)(2,1)} %get-tuple-element.57) | copy-start | bytes 4718596
  295.0 2.2 copy-start.10
  295.0 2.8 copy-start.11
  295.0 3.4 %copy-start.9 = (f32[96,192]{1,0:T(8,128)S(1)}, f32[96,192]{1,0:T(8,128)}, u32[]{:S(2)}) copy-start(f32[96,192]{1,0:T(8,128)} %get-tuple-element.92) | copy-start | bytes 221188
  295.0 4.1 %copy-start.8 = (f32[96,768]{1,0:T(8,128)S(1)}, f32[96,768]{1,0:T(8,128)}, u32[]{:S(2)}) copy-start(f32[96,768]{1,0:T(8,128)} %get-tuple-element.93) | copy-start | bytes 884740
  295.1 4.8 %copy-start.7 = (f32[96,768]{1,0:T(8,128)S(1)}, f32[96,768]{1,0:T(8,128)}, u32[]{:S(2)}) copy-start(f32[96,768]{1,0:T(8,128)} %get-tuple-element.94) | copy-start | bytes 884740
